TPU v7x, 512 devices: a whole 4x8x8 slice. The times are simulated.
512 devices in a mesh: grid: 32 (over y, z_lo), row: 4 (over x), col: 4 (over z_hi, core).
Axes of the slice: x: 4, y: 8, z: 8 (z_hi: 2, z_lo: 4; z = z_hi * 4 + z_lo), core: 2. Of those that a mesh axis runs over, the one named last changes fastest.
Arguments:
- schur: bfloat16 [32, 4096, 4096], P('grid', 'row', 'col'), may hold values from -6 to 6
- d_inv: bfloat16 [3, 32, 1024, 1024], P(None, 'grid', None, 'col'), may hold values from -0.0009765625 to 0.0087890625, as said below
- blocks: int32 [3, 32, 12], P(None, 'grid'), may hold values from 0 to 15, as said below
Outputs:
- merged: bfloat16 [32, 512, 4096], P('grid', 'row', 'col')
Inputs may be any that keep to these rules, and one draw needn't show every extreme that they name: blocks[l, g] is the same for all grids g of one group of 2^l grids at level l. Entry k < 4 lies in k * 4 to (k + 1) * 4 - 1; the other 8 entries are distinct blocks, none of them a pivot block of that list. d_inv[l, g] is the same for all grids g of one group of 2^l grids at level l.
All inputs are finite; a program needn't handle non-finite values.
Results may differ from a plain program's by a relative error of at most 0.0067.
Values may be sent and summed in bfloat16 or wider, within the bound.
No kernel may reach another device: no remote copies, remote signals or barrier semaphores. Data moves between devices by JAX's collectives and lax.ppermute only.
A program may use at most 64 MiB of HBM per device.

v0:
```python
import jax
import jax.numpy as jnp
from jax import lax
from jax.sharding import PartitionSpec as P


def swapped(block, axis, apart):
    count = lax.axis_size(axis)
    route = []
    for low in range(count):
        high = low | 1 << apart
        if high != low and high < count:
            route += [(low, high), (high, low)]
    return lax.ppermute(block, axis, route)


def unchanged(tile_rows, other_rows):
    return tile_rows


def shards(schur, d_inv, blocks):
    n_rows = lax.axis_size("row")
    grid_pos = lax.axis_index("grid")
    row_pos = lax.axis_index("row")
    col_pos = lax.axis_index("col")
    levels = blocks.shape[0]
    current = schur[0].astype(jnp.float32)
    quarter_rows = current.shape[0]
    local_cols = current.shape[1]
    width = d_inv.shape[2]
    block = width // n_rows
    col_start = col_pos * local_cols
    col_ids = (col_start + jnp.arange(local_cols, dtype=jnp.int32)) // block
    row_shift = jnp.zeros((), jnp.int32)
    for height in range(levels):
        rows_here = current.shape[0]
        count = rows_here // block
        chosen = blocks[height, 0]
        pivots = chosen[:n_rows]
        listed = chosen[n_rows:]
        row_start = row_pos * quarter_rows + row_shift
        col_keep = jnp.any(col_ids[:, None] == listed[None, :], axis=1)
        row_ids = row_start // block + jnp.arange(count, dtype=jnp.int32)
        row_keep = jnp.any(row_ids[:, None] == listed[None, :], axis=1)
        left_piece = lax.dynamic_slice_in_dim(
            current, pivots[col_pos] * block - col_start, block, 1
        ).astype(jnp.bfloat16)
        left_panel = lax.all_gather(left_piece, "col", axis=1, tiled=True)
        offset = pivots[row_pos] * block - row_start
        owned = (offset >= 0) & (offset < rows_here)
        upper_piece = lax.dynamic_slice_in_dim(
            current, jnp.clip(offset, 0, rows_here - block), block, 0
        )
        upper_piece = jnp.where(owned, upper_piece, 0.0).astype(jnp.bfloat16)
        for member_bit in range(height):
            upper_piece = upper_piece + swapped(upper_piece, "grid", member_bit)
        upper_panel = lax.all_gather(upper_piece, "row", axis=0, tiled=True)
        upper_panel = jnp.where(col_keep[None, :], upper_panel, jnp.zeros((), jnp.bfloat16))
        inverse_part = d_inv[height, 0]
        pieces = []
        inverse_full = lax.all_gather(inverse_part, "col", axis=1, tiled=True)

        def update_block(tile_rows, left_rows):
            scaled = jnp.dot(left_rows, inverse_full, preferred_element_type=jnp.float32).astype(
                jnp.bfloat16
            )
            return tile_rows - jnp.dot(scaled, upper_panel, preferred_element_type=jnp.float32)

        for position in range(count):
            tile_rows = current[position * block : (position + 1) * block]
            left_rows = left_panel[position * block : (position + 1) * block]
            pieces.append(
                lax.cond(row_keep[position], update_block, unchanged, tile_rows, left_rows)
            )
        updated = jnp.concatenate(pieces, axis=0).astype(jnp.bfloat16)
        bit_value = grid_pos >> height & 1
        half_rows = rows_here // 2
        kept = lax.dynamic_slice_in_dim(updated, bit_value * half_rows, half_rows, 0)
        given = lax.dynamic_slice_in_dim(updated, (1 - bit_value) * half_rows, half_rows, 0)
        received = swapped(given, "grid", height)
        current = kept.astype(jnp.float32) + received.astype(jnp.float32)
        row_shift = row_shift + bit_value * half_rows
    return current.astype(jnp.bfloat16)[None]


def solution(mesh):
    return jax.shard_map(
        shards,
        mesh=mesh,
        in_specs=(P("grid", "row", "col"), P(None, "grid", None, "col"), P(None, "grid", None)),
        out_specs=P("grid", "row", "col"),
        check_vma=False,
    )
```

profile of v0, /device:TPU:16, one launch (start us, length us, event | category | flops | bytes accessed | tf_op | source)
XLA Modules:
  0.0 482.4 jit_solution(4300565674593944556)
XLA Ops:
  8.5 4.0 convert_element_type.125
  12.5 2.3 select_convert_fusion.2
  15.5 2.1 dynamic-slice_convert_fusion
  22.5 3.6 slice_bitcast_fusion.3
  26.0 29.5 %all-gather.24.cloned.1.call-done = bf16[1,1024,1024]{2,1,0:T(8,128)(2,1)} async-done(((bf16[1,256,1024]{2,1,0:T(8,128)(2,1)}), bf16[1,1024,1024]{2,1,0:T(8,128)(2,1)}) %all-gather.24.cloned.1.call-update) | async-done | bytes 2097168 | tf_op jit(solution)/shard_map/all_gather | solution.py:57
  55.6 3.1 bitcast_select_fusion
  58.7 45.7 %all-gather.20.cloned.1.call-done = bf16[1,1024,1024]{2,1,0:T(8,128)(2,1)} async-done(((bf16[1,1024,256]{2,1,0:T(8,128)(2,1)}), bf16[1,1024,1024]{2,1,0:T(8,128)(2,1)}) %all-gather.20.cloned.1.call-update) | async-done | bytes 2097168 | tf_op jit(solution)/shard_map/all_gather | solution.py:48
  104.4 45.0 %all-gather.22.cloned.1.call-done = bf16[1,1,1024,1024]{3,2,1,0:T(8,128)(2,1)} async-done(((bf16[1,1,1024,256]{3,2,1,0:T(8,128)(2,1)}), bf16[1,1,1024,1024]{3,2,1,0:T(8,128)(2,1)}) %all-gather.22.cloned.1.call-update) | async-done | bytes 2097168 | tf_op jit(solution)/shard_map/all_gather | solution.py:61
  149.4 2.1 convert.24
  155.3 7.1 %collective-permute-start = (bf16[512,1024]{1,0:T(8,128)(2,1)S(1)}, bf16[512,1024]{1,0:T(8,128)(2,1)S(1)}, u32[]{:S(2)}, u32[]{:S(2)}) collective-permute-start(bf16[512,1024]{1,0:T(8,128)(2,1)S(1)} %constant_dynamic-slice_fusion.5), channel_id=1, source_target_pairs={{0,16},{16,0},{32,48},{48,32},{64,80},{80,64},{96,112},{112,96},{1... | collective-permute-start | bytes 3145736 | tf_op jit(solution)/shard_map/ppermute | solution.py:14
  163.7 22.2 %collective-permute-done = bf16[512,1024]{1,0:T(8,128)(2,1)S(1)} collective-permute-done((bf16[512,1024]{1,0:T(8,128)(2,1)S(1)}, bf16[512,1024]{1,0:T(8,128)(2,1)S(1)}, u32[]{:S(2)}, u32[]{:S(2)}) %collective-permute-start) | collective-permute-done | bytes 1048608 | tf_op jit(solution)/shard_map/ppermute | solution.py:14
  185.9 1.6 convert_add_fusion
  187.7 3.6 collective-permute-start.1
  191.3 11.7 %collective-permute-done.1 = bf16[256,1024]{1,0:T(8,128)(2,1)S(1)} collective-permute-done((bf16[256,1024]{1,0:T(8,128)(2,1)S(1)}, bf16[256,1024]{1,0:T(8,128)(2,1)S(1)}, u32[]{:S(2)}, u32[]{:S(2)}) %collective-permute-start.1) | collective-permute-done | bytes 524320 | tf_op jit(solution)/shard_map/ppermute | solution.py:14
  210.2 34.5 %all-gather.16.cloned.1.call-done = bf16[1024,1024]{1,0:T(8,128)(2,1)} async-done(((bf16[256,1024]{1,0:T(8,128)(2,1)}), bf16[1024,1024]{1,0:T(8,128)(2,1)}) %all-gather.16.cloned.1.call-update) | async-done | bytes 2097168 | tf_op jit(solution)/shard_map/all_gather | solution.py:57
  244.7 3.2 broadcast_select_fusion
  247.9 45.4 %all-gather.26.cloned.1.call-done = bf16[1,1,1024,1024]{3,2,1,0:T(8,128)(2,1)} async-done(((bf16[1,1,1024,256]{3,2,1,0:T(8,128)(2,1)}), bf16[1,1,1024,1024]{3,2,1,0:T(8,128)(2,1)}) %all-gather.26.cloned.1.call-update) | async-done | bytes 2097168 | tf_op jit(solution)/shard_map/all_gather | solution.py:61
  293.4 33.2 %all-gather.14.cloned.1.call-done = bf16[512,1024]{1,0:T(8,128)(2,1)} async-done(((bf16[512,256]{1,0:T(8,128)(2,1)}), bf16[512,1024]{1,0:T(8,128)(2,1)}) %all-gather.14.cloned.1.call-update) | async-done | bytes 1048592 | tf_op jit(solution)/shard_map/all_gather | solution.py:48
  326.6 3.7 conditional.11
  326.7 3.7 convolution_subtract_fusion.4
  331.0 2.2 collective-permute-start.2
  333.9 47.7 %collective-permute-done.2 = bf16[256,1024]{1,0:T(8,128)(2,1)S(1)} collective-permute-done((bf16[256,1024]{1,0:T(8,128)(2,1)S(1)}, bf16[256,1024]{1,0:T(8,128)(2,1)S(1)}, u32[]{:S(2)}, u32[]{:S(2)}) %collective-permute-start.2) | collective-permute-done | bytes 524320 | tf_op jit(solution)/shard_map/ppermute | solution.py:14
  382.2 2.1 collective-permute-start.3
  384.3 13.0 %collective-permute-done.3 = bf16[256,1024]{1,0:T(8,128)(2,1)S(1)} collective-permute-done((bf16[256,1024]{1,0:T(8,128)(2,1)S(1)}, bf16[256,1024]{1,0:T(8,128)(2,1)S(1)}, u32[]{:S(2)}, u32[]{:S(2)}) %collective-permute-start.3) | collective-permute-done | bytes 524320 | tf_op jit(solution)/shard_map/ppermute | solution.py:14
  397.5 2.6 collective-permute-start.4
  400.1 23.8 %collective-permute-done.4 = bf16[256,1024]{1,0:T(8,128)(2,1)S(1)} collective-permute-done((bf16[256,1024]{1,0:T(8,128)(2,1)S(1)}, bf16[256,1024]{1,0:T(8,128)(2,1)S(1)}, u32[]{:S(2)}, u32[]{:S(2)}) %collective-permute-start.4) | collective-permute-done | bytes 524320 | tf_op jit(solution)/shard_map/ppermute | solution.py:14
  427.0 11.5 %all_gather.33 = bf16[256,1024]{1,0:T(8,128)(2,1)} all-gather(bf16[256,256]{1,0:T(8,128)(2,1)S(1)} %dynamic-slice_convert_fusion.2), channel_id=1, replica_groups=mesh['grid'=32,'row'=4,'col'=4] {'col'}, dimensions={1}, use_global_device_ids=true | all-gather | bytes 655360 | tf_op jit(solution)/shard_map/all_gather | solution.py:48
  438.5 22.3 %all-gather.18.cloned.1.call-done = bf16[1024,1024]{1,0:T(8,128)(2,1)} async-done(((bf16[256,1024]{1,0:T(8,128)(2,1)}), bf16[1024,1024]{1,0:T(8,128)(2,1)}) %all-gather.18.cloned.1.call-update) | async-done | bytes 2097168 | tf_op jit(solution)/shard_map/all_gather | solution.py:57
  461.1 3.8 conditional.13
  461.2 3.7 fusion.15
  465.0 1.9 collective-permute-start.5
  466.9 7.8 %collective-permute-done.5 = bf16[128,1024]{1,0:T(8,128)(2,1)S(1)} collective-permute-done((bf16[128,1024]{1,0:T(8,128)(2,1)S(1)}, bf16[128,1024]{1,0:T(8,128)(2,1)S(1)}, u32[]{:S(2)}, u32[]{:S(2)}) %collective-permute-start.5) | collective-permute-done | bytes 262176 | tf_op jit(solution)/shard_map/ppermute | solution.py:14
  (69 shorter events, 17.8 us)
Async XLA Ops:
  6.5 49.0 %all-gather.24.cloned.1.call-start = ((), (), s32[]{:S(2)}) async-start(), calls=%async_computation.5 | async-start | bytes 2621440 | tf_op jit(solution)/shard_map/all_gather | solution.py:57
  12.5 5.1 %copy-start.4 = (bf16[3,1,1024,256]{3,2,1,0:T(8,128)(2,1)S(1)}, bf16[3,1,1024,256]{3,2,1,0:T(8,128)(2,1)}, u32[]{:S(2)}) copy-start(bf16[3,1,1024,256]{3,2,1,0:T(8,128)(2,1)} %param.18) | copy-start | bytes 4718596
  14.8 89.5 %all-gather.20.cloned.1.call-start = ((), (), s32[]{:S(2)}) async-start(), calls=%async_computation.3 | async-start | bytes 2621440 | tf_op jit(solution)/shard_map/all_gather | solution.py:48
  17.6 1.4 copy-start.5
  17.6 131.8 %all-gather.22.cloned.1.call-start = ((), (), s32[]{:S(2)}) async-start(), calls=%async_computation.4 | async-start | bytes 2621440 | tf_op jit(solution)/shard_map/all_gather | solution.py:61
  18.9 225.8 %all-gather.16.cloned.1.call-start = ((), (), s32[]{:S(2)}) async-start(), calls=%async_computation.1 | async-start | bytes 2621440 | tf_op jit(solution)/shard_map/all_gather | solution.py:57
  152.5 1.0 copy-start.2
  152.5 1.2 copy-start.3
  153.8 1.4 copy-start
  155.3 30.6 %collective-permute-start = (bf16[512,1024]{1,0:T(8,128)(2,1)S(1)}, bf16[512,1024]{1,0:T(8,128)(2,1)S(1)}, u32[]{:S(2)}, u32[]{:S(2)}) collective-permute-start(bf16[512,1024]{1,0:T(8,128)(2,1)S(1)} %constant_dynamic-slice_fusion.5), channel_id=1, source_target_pairs={{0,16},{16,0},{32,48},{48,32},{64,80},{80,64},{96,112},{112,96},{1... | collective-permute-start | bytes 3145736 | tf_op jit(solution)/shard_map/ppermute | solution.py:14
  187.7 15.4 %collective-permute-start.1 = (bf16[256,1024]{1,0:T(8,128)(2,1)S(1)}, bf16[256,1024]{1,0:T(8,128)(2,1)S(1)}, u32[]{:S(2)}, u32[]{:S(2)}) collective-permute-start(bf16[256,1024]{1,0:T(8,128)(2,1)S(1)} %select_convert_fusion.1), channel_id=1, source_target_pairs={{0,16},{16,0},{32,48},{48,32},{64,80},{80,64},{96,112},{112,96},{1... | collective-permute-start | bytes 1572872 | tf_op jit(solution)/shard_map/ppermute | solution.py:14
  204.1 89.3 %all-gather.26.cloned.1.call-start = ((), (), s32[]{:S(2)}) async-start(), calls=%async_computation.6 | async-start | bytes 2621440 | tf_op jit(solution)/shard_map/all_gather | solution.py:61
  204.7 121.9 %all-gather.14.cloned.1.call-start = ((), (), s32[]{:S(2)}) async-start(), calls=%async_computation | async-start | bytes 1310720 | tf_op jit(solution)/shard_map/all_gather | solution.py:48
  206.1 232.4 %all-gather.28.cloned.1.call-start = ((), (), s32[]{:S(2)}) async-start(), calls=%async_computation.7 | async-start | bytes 2621440 | tf_op jit(solution)/shard_map/all_gather | solution.py:61
  206.9 253.9 %all-gather.18.cloned.1.call-start = ((), (), s32[]{:S(2)}) async-start(), calls=%async_computation.2 | async-start | bytes 2621440 | tf_op jit(solution)/shard_map/all_gather | solution.py:57
  244.7 81.8 %copy-start.1 = (f32[256,1024]{1,0:T(8,128)S(1)}, f32[256,1024]{1,0:T(8,128)}, u32[]{:S(2)}) copy-start(f32[256,1024]{1,0:T(8,128)} %get-tuple-element.154) | copy-start | bytes 3145732
  331.0 50.6 %collective-permute-start.2 = (bf16[256,1024]{1,0:T(8,128)(2,1)S(1)}, bf16[256,1024]{1,0:T(8,128)(2,1)S(1)}, u32[]{:S(2)}, u32[]{:S(2)}) collective-permute-start(bf16[256,1024]{1,0:T(8,128)(2,1)S(1)} %fusion.18), channel_id=1, source_target_pairs={{0,32},{32,0},{16,48},{48,16},{64,96},{96,64},{80,112},{112,80},{1... | collective-permute-start | bytes 1572872 | tf_op jit(solution)/shard_map/ppermute | solution.py:14
  382.2 15.1 %collective-permute-start.3 = (bf16[256,1024]{1,0:T(8,128)(2,1)S(1)}, bf16[256,1024]{1,0:T(8,128)(2,1)S(1)}, u32[]{:S(2)}, u32[]{:S(2)}) collective-permute-start(bf16[256,1024]{1,0:T(8,128)(2,1)S(1)} %get-tuple-element.148), channel_id=1, source_target_pairs={{0,16},{16,0},{32,48},{48,32},{64,80},{80,64},{96,112},{112,96},{1... | collective-permute-start | bytes 1572872 | tf_op jit(solution)/shard_map/ppermute | solution.py:14
  397.5 26.4 %collective-permute-start.4 = (bf16[256,1024]{1,0:T(8,128)(2,1)S(1)}, bf16[256,1024]{1,0:T(8,128)(2,1)S(1)}, u32[]{:S(2)}, u32[]{:S(2)}) collective-permute-start(bf16[256,1024]{1,0:T(8,128)(2,1)S(1)} %add.129), channel_id=1, source_target_pairs={{0,32},{32,0},{16,48},{48,16},{64,96},{96,64},{80,112},{112,80},{1... | collective-permute-start | bytes 1572872 | tf_op jit(solution)/shard_map/ppermute | solution.py:14
  465.0 9.8 %collective-permute-start.5 = (bf16[128,1024]{1,0:T(8,128)(2,1)S(1)}, bf16[128,1024]{1,0:T(8,128)(2,1)S(1)}, u32[]{:S(2)}, u32[]{:S(2)}) collective-permute-start(bf16[128,1024]{1,0:T(8,128)(2,1)S(1)} %constant_dynamic-slice_fusion), channel_id=1, source_target_pairs={{0,64},{64,0},{16,80},{80,16},{32,96},{96,32},{48,112},{112,48},{1... | collective-permute-start | bytes 786440 | tf_op jit(solution)/shard_map/ppermute | solution.py:14
Sparse Core Ops, SparseCore 0:
  15.0 40.5 all-gather.23
  57.7 46.6 all-gather.19
  106.5 42.8 all-gather.21
  204.2 40.4 all-gather.15
  246.7 46.6 all-gather.25
  295.3 31.1 all-gather.13
  328.6 42.9 all-gather.27
  425.0 35.7 all-gather.17
where the time goes:
time: 483 us; the launch traced here: 482 us
  waiting for transfers between devices  383 us (79%)
  other arithmetic  23.3 us (5%)
  between operations  22.1 us (5%)
  starting transfers between devices  19.9 us (4%)
  local copies, waits for them, and re-layouts  14.9 us (3%)
  blocking collectives  11.5 us (2%)
  matrix products  7.43 us (2%)
    ppermute x6, waiting for transfers between devices, swapped(): return lax.ppermute(block, axis, route)  126 us
    all_gather x3, waiting for transfers between devices, shards(): inverse_full = lax.all_gather(inverse_part, 'col', axis=1, tiled=True)  90.4 us
    all_gather x3, waiting for transfers between devices, shards(): upper_panel = lax.all_gather(upper_piece, 'row', axis=0, tiled=True)  86.3 us
    all_gather x2, waiting for transfers between devices, shards(): left_panel = lax.all_gather(left_piece, 'col', axis=1, tiled=True)  78.9 us
    ppermute x6, starting transfers between devices, swapped(): return lax.ppermute(block, axis, route)  19.6 us
    all_gather x1, blocking collectives, shards(): left_panel = lax.all_gather(left_piece, 'col', axis=1, tiled=True)  11.5 us
  transfers between devices with their start and end apart: 14, of which 13 were waited for; matrix products, arithmetic and copies ran while one was open for 5% of the time, Pallas kernels for 0%

commit v1 on v0

v1 whole, which is shorter than its diff:
```python
import jax
import jax.numpy as jnp
from jax import lax
from jax.experimental import pallas as pl
from jax.experimental.pallas import tpu as pltpu
from jax.sharding import PartitionSpec as P


BF = jnp.bfloat16
F32 = jnp.float32


def move(block, axes, route):
    sizes = [lax.axis_size(a) for a in axes]
    count = 1
    for s in sizes:
        count *= s
    return lax.ppermute(block, axes, [(i, route(i)) for i in range(count)])


def across(block, apart):
    return move(block, ("grid",), lambda i: i ^ apart)


def far_half(block):
    return move(block, ("col",), lambda i: i ^ 2)


def other_core(block):
    return move(block, ("col",), lambda i: i ^ 1)


def row_swap(block, first):
    cols = lax.axis_size("col")

    def route(i):
        r, c = divmod(i, cols)
        mask = 1 if (c % 2 == 0) == first else 3
        return (r ^ mask) * cols + c

    return move(block, ("row", "col"), route)


def arrival(quarter, row, core):
    x = quarter ^ row
    near = jnp.where(core == 0, 1, 3)
    return jnp.where(x == 0, 0, jnp.where(x == 2, 3, jnp.where(x == near, 1, 2)))


def has(blk, level, wanted):
    found = blk[level, 4] == wanted
    for n in range(5, 12):
        found = found | (blk[level, n] == wanted)
    return found


def slot_of(b, pivot):
    return jnp.clip(b - jnp.where(b > pivot, 1, 0), 0, 2)


def block_of(slot, pivot):
    return slot + jnp.where(slot >= pivot, 1, 0)


def row_pivot(blk, pos, level):
    return blk[level, pos[1]] - 4 * pos[1]


def col_pivot(blk, pos, level):
    return blk[level, pos[2]] - 4 * pos[2]


def bit_of(pos, n):
    return (pos[0] >> n) & 1


def call(body, grid, in_specs, out_specs, out_shape, scratch, flops=0, size=0):
    return pl.pallas_call(
        body,
        grid_spec=pltpu.PrefetchScalarGridSpec(
            num_scalar_prefetch=2,
            grid=grid,
            in_specs=in_specs,
            out_specs=out_specs,
            scratch_shapes=scratch,
        ),
        out_shape=out_shape,
        compiler_params=pltpu.CompilerParams(
            dimension_semantics=("arbitrary",) * len(grid), vmem_limit_bytes=32 * 2**20
        ),
        cost_estimate=pl.CostEstimate(flops=flops, bytes_accessed=size, transcendentals=0),
    )


def whole(shape):
    return pl.BlockSpec(shape, lambda *_: (0,) * len(shape))


def out(shape):
    return jax.ShapeDtypeStruct(shape, BF)


def pack(blk, pos, tile):
    def body(blk_ref, pos_ref, left_in, upper_in, left_out, upper_out):
        left_out[0] = left_in[0]
        upper_out[0] = upper_in[0]

    spec = pl.BlockSpec((1, 256, 256), lambda i, blk, pos: (i, 0, 0))
    return call(
        body,
        (3,),
        [
            pl.BlockSpec(
                (1, 256, 256),
                lambda i, blk, pos: (0, block_of(i, row_pivot(blk, pos, 0)), col_pivot(blk, pos, 0)),
            ),
            pl.BlockSpec(
                (1, 256, 256),
                lambda i, blk, pos: (0, row_pivot(blk, pos, 0), block_of(i, col_pivot(blk, pos, 0))),
            ),
        ],
        [spec, spec],
        [out((3, 256, 256)), out((3, 256, 256))],
        [],
        size=2**20,
    )(blk, pos, tile, tile)


def join_inverse(blk, pos, levels, own, far, other, other_far):
    first, count = levels

    def body(blk_ref, pos_ref, dc, dz, oc, oz, d_ref):
        c = pos_ref[2]
        for flip, ref in zip((0, 2, 1, 3), (dc, dz, oc, oz)):
            d_ref[0, :, pl.ds(pl.multiple_of((c ^ flip) * 256, 256), 256)] = ref[0, 0]

    def far_map(flip):
        return lambda n, k, blk, pos: (arrival(k, pos[1], pos[2] % 2 ^ flip), n, 0, 0)

    near = pl.BlockSpec((1, 1, 256, 256), lambda n, k, blk, pos: (first + n, k, 0, 0))
    return call(
        body,
        (count, 4),
        [
            near,
            pl.BlockSpec((1, 1, 256, 256), far_map(0)),
            near,
            pl.BlockSpec((1, 1, 256, 256), far_map(1)),
        ],
        pl.BlockSpec((1, 256, 1024), lambda n, k, blk, pos: (n, k, 0)),
        out((count, 1024, 1024)),
        [],
        size=count * 2**22,
    )(blk, pos, own, far, other, other_far)


def join_upper(blk, pos, pieces):
    parts = len(pieces)
    rows = 256 // parts

    def body(blk_ref, pos_ref, *refs):
        u_all = refs[-1]
        r, c = pos_ref[1], pos_ref[2]
        near_q = r ^ jnp.where(c % 2 == 0, 1, 3)
        far_q = r ^ jnp.where(c % 2 == 0, 3, 1)
        for h in range(parts):
            u0, u1, u2 = refs[3 * h : 3 * h + 3]
            for s in range(3):
                u_all[s, pl.ds(r * 256 + h * rows, rows)] = u0[s]
                u_all[s, pl.ds(near_q * 256 + h * rows, rows)] = u1[s]
                u_all[s, pl.ds(far_q * 256 + h * rows, rows)] = u2[0, s]
                u_all[s, pl.ds((r ^ 2) * 256 + h * rows, rows)] = u2[1, s]

    return call(
        body,
        (1,),
        [whole((3, rows, 256)), whole((3, rows, 256)), whole((2, 3, rows, 256))] * parts,
        whole((3, 1024, 256)),
        out((3, 1024, 256)),
        [],
        size=3 * 2**20,
    )(blk, pos, *[x for piece in pieces for x in piece])


def scale(blk, pos, lane, lefts, inverse):
    rows = lefts[0].shape[0]

    def body(blk_ref, pos_ref, l0, l1, l2, l3, d_ref, s_ref, l_all):
        c = pos_ref[2]

        @pl.when(pl.program_id(0) == 0)
        def _():
            for flip, ref in zip((0, 2, 1, 3), (l0, l1, l2, l3)):
                for i in range(rows):
                    l_all[i * 256 : (i + 1) * 256, pl.ds(pl.multiple_of((c ^ flip) * 256, 256), 256)] = ref[i]

        s_ref[...] = jnp.dot(l_all[...], d_ref[0], preferred_element_type=F32).astype(BF)

    return call(
        body,
        (4,),
        [whole((rows, 256, 256))] * 4
        + [pl.BlockSpec((1, 1024, 256), lambda q, blk, pos: (lane, 0, q))],
        pl.BlockSpec((rows * 256, 256), lambda q, blk, pos: (0, q)),
        out((rows * 256, 1024)),
        [pltpu.VMEM((rows * 256, 1024), BF)],
        flops=2 * rows * 256 * 1024 * 1024,
        size=4 * 2**20,
    )(blk, pos, *lefts, inverse)


def subtract_product(blk_ref, pos_ref, level, row_block, scaled, u_ref, e_all, held):
    c = pos_ref[2]
    pivot = col_pivot(blk_ref, pos_ref, level)
    row_on = has(blk_ref, level, pos_ref[1] * 4 + row_block)
    for s in range(3):
        b = block_of(s, pivot)
        on = row_on & has(blk_ref, level, c * 4 + b)

        @pl.when(on)
        def _():
            change = jnp.dot(scaled(), u_ref[s], preferred_element_type=F32)
            e_all[b] = (held(b, s) - change).astype(BF)

        @pl.when(jnp.logical_not(on))
        def _():
            e_all[b] = held(b, s).astype(BF)


def update_first(blk, pos, tile, scaled, upper):
    def row_block(i, pos):
        bit = bit_of(pos, 0)
        return jnp.where(i < 2, 2 * (1 - bit), 2 * bit) + (i & 1)

    def body(blk_ref, pos_ref, x_ref, s_ref, u_ref, a0, a1, al, b0, b1, ks, kp, e_all):
        i = pl.program_id(0)
        rb = row_block(i, pos_ref)
        for b in range(4):
            e_all[b] = x_ref[0, :, b * 256 : (b + 1) * 256]
        subtract_product(
            blk_ref, pos_ref, 0, rb, lambda: s_ref[...], u_ref, e_all,
            lambda b, s: e_all[b].astype(F32),
        )
        nxt = col_pivot(blk_ref, pos_ref, 1)
        half = i & 1

        for n, b_ref in ((0, b0), (1, b1)):

            @pl.when(i == n)
            def _():
                al[n] = e_all[nxt]
                for d in range(3):
                    b_ref[d] = e_all[block_of(d, nxt)]

        @pl.when(i >= 2)
        def _():
            kp[half] = e_all[nxt]
            for d in range(3):
                ks[half, d] = e_all[block_of(d, nxt)]

        @pl.when(rb == row_pivot(blk_ref, pos_ref, 1))
        def _():
            for d in range(3):
                a0[d] = e_all[block_of(d, nxt), :128]
                a1[d] = e_all[block_of(d, nxt), 128:]

    shapes = [
        (3, 128, 256), (3, 128, 256), (2, 256, 256), (3, 256, 256), (3, 256, 256),
        (2, 3, 256, 256), (2, 256, 256),
    ]
    return call(
        body,
        (4,),
        [
            pl.BlockSpec((1, 256, 1024), lambda i, blk, pos: (0, row_block(i, pos), 0)),
            pl.BlockSpec(
                (256, 1024),
                lambda i, blk, pos: (slot_of(row_block(i, pos), row_pivot(blk, pos, 0)), 0),
            ),
            whole((3, 1024, 256)),
        ],
        [whole(x) for x in shapes],
        [out(x) for x in shapes],
        [pltpu.VMEM((4, 256, 256), BF)],
        flops=2 * 768 * 1024 * 768,
        size=8 * 2**20,
    )(blk, pos, tile, scaled, upper)


def update_second(blk, pos, ks, rb0, rb1, kp, ra, scaled, upper):
    def body(
        blk_ref, pos_ref, ks_ref, rb0_ref, rb1_ref, kp_ref, ra_ref, s_ref, u_ref,
        a0, a1, al, bg, ks2, kp2, e_all,
    ):
        pivot = col_pivot(blk_ref, pos_ref, 1)
        nxt = col_pivot(blk_ref, pos_ref, 2)
        for d in range(3):
            a0[d] = jnp.zeros((128, 256), BF)
            a1[d] = jnp.zeros((128, 256), BF)
        for n, rb_ref in ((0, rb0_ref), (1, rb1_ref)):
            here = 2 * bit_of(pos_ref, 0) + n
            e_all[pivot] = (kp_ref[n].astype(F32) + ra_ref[n].astype(F32)).astype(BF)
            subtract_product(
                blk_ref, pos_ref, 1, here, lambda: s_ref[n * 256 : (n + 1) * 256], u_ref, e_all,
                lambda b, s: ks_ref[n, s].astype(F32) + rb_ref[s].astype(F32),
            )

            @pl.when(bit_of(pos_ref, 1) != n)
            def _():
                al[0] = e_all[nxt]
                for d in range(3):
                    bg[d] = e_all[block_of(d, nxt)]

            @pl.when(bit_of(pos_ref, 1) == n)
            def _():
                kp2[0] = e_all[nxt]
                for d in range(3):
                    ks2[d] = e_all[block_of(d, nxt)]

            @pl.when(here == row_pivot(blk_ref, pos_ref, 2))
            def _():
                for d in range(3):
                    a0[d] = e_all[block_of(d, nxt), :128]
                    a1[d] = e_all[block_of(d, nxt), 128:]

    shapes = [
        (3, 128, 256), (3, 128, 256), (1, 256, 256), (3, 256, 256), (3, 256, 256), (1, 256, 256),
    ]
    return call(
        body,
        (1,),
        [whole(x.shape) for x in (ks, rb0, rb1, kp, ra, scaled, upper)],
        [whole(x) for x in shapes],
        [out(x) for x in shapes],
        [pltpu.VMEM((4, 256, 256), BF)],
        flops=2 * 512 * 1024 * 768,
        size=7 * 2**20,
    )(blk, pos, ks, rb0, rb1, kp, ra, scaled, upper)


def update_third(blk, pos, ks, rb, kp, ra, scaled, upper):
    def body(
        blk_ref, pos_ref, ks_ref, rb_ref, kp_ref, ra_ref, s_ref, u_ref, give, keep, e_all
    ):
        here = 2 * bit_of(pos_ref, 0) + bit_of(pos_ref, 1)
        pivot = col_pivot(blk_ref, pos_ref, 2)
        e_all[pivot] = (kp_ref[0].astype(F32) + ra_ref[0].astype(F32)).astype(BF)
        subtract_product(
            blk_ref, pos_ref, 2, here, lambda: s_ref[...], u_ref, e_all,
            lambda b, s: ks_ref[s].astype(F32) + rb_ref[s].astype(F32),
        )
        bit = bit_of(pos_ref, 2)
        for b in range(4):
            give[:, b * 256 : (b + 1) * 256] = e_all[b, pl.ds((1 - bit) * 128, 128)]
            keep[:, b * 256 : (b + 1) * 256] = e_all[b, pl.ds(bit * 128, 128)]

    return call(
        body,
        (1,),
        [whole(x.shape) for x in (ks, rb, kp, ra, scaled, upper)],
        [whole((128, 1024)), whole((128, 1024))],
        [out((128, 1024)), out((128, 1024))],
        [pltpu.VMEM((4, 256, 256), BF)],
        flops=2 * 256 * 1024 * 768,
        size=4 * 2**20,
    )(blk, pos, ks, rb, kp, ra, scaled, upper)


def total(a, b):
    return (a.astype(F32) + b.astype(F32)).astype(BF)


def spread_rows(piece):
    near = row_swap(piece, True)
    far = row_swap(jnp.stack([piece, near]), False)
    return piece, near, far


def gather_left(piece):
    far = far_half(piece)
    own_other = other_core(piece)
    far_other = other_core(far)
    return piece, far, own_other, far_other


def far_inverse(part):
    arrived = far_half(part)
    near = row_swap(arrived, True)
    two = jnp.stack([arrived, near])
    four = jnp.concatenate([two, row_swap(two, False)])
    return four, other_core(four)


def eliminate(schur, d_inv, blocks):
    row = lax.axis_index("row").astype(jnp.int32)
    blk = blocks[:, 0]
    pos = jnp.stack(
        [lax.axis_index("grid").astype(jnp.int32), row, lax.axis_index("col").astype(jnp.int32)]
    )
    inverse = d_inv.reshape(3, 4, 256, 256)
    quarter = lax.dynamic_index_in_dim(inverse, row, 1, keepdims=False)

    dz0, oz0 = far_inverse(quarter[:1])
    left0, upper0 = pack(blk, pos, schur)
    d_other = other_core(inverse)
    upper0 = join_upper(blk, pos, [spread_rows(upper0)])
    lefts0 = gather_left(left0)
    dz12, oz12 = far_inverse(quarter[1:])
    whole0 = join_inverse(blk, pos, (0, 1), inverse, dz0, d_other, oz0)
    whole12 = join_inverse(blk, pos, (1, 2), inverse, dz12, d_other, oz12)

    scaled0 = scale(blk, pos, 0, lefts0, whole0)
    a0, a1, al, b0, b1, ks, kp = update_first(blk, pos, schur, scaled0, upper0)
    u10 = total(a0, across(a0, 1))
    ral = across(al, 1)
    u11 = total(a1, across(a1, 1))
    rb0 = across(b0, 1)
    rb1 = across(b1, 1)
    upper1 = join_upper(blk, pos, [spread_rows(u10), spread_rows(u11)])
    lefts1 = gather_left(total(kp, ral))
    scaled1 = scale(blk, pos, 0, lefts1, whole12)
    a0, a1, al, bg, ks, kp = update_second(blk, pos, ks, rb0, rb1, kp, ral, scaled1, upper1)

    u20 = total(a0, across(a0, 2))
    u21 = total(a1, across(a1, 2))
    ral = across(al, 2)
    rb = across(bg, 2)
    u20 = total(u20, across(u20, 1))
    u21 = total(u21, across(u21, 1))
    upper2 = join_upper(blk, pos, [spread_rows(u20), spread_rows(u21)])
    lefts2 = gather_left(total(kp, ral))
    scaled2 = scale(blk, pos, 1, lefts2, whole12)
    give, keep = update_third(blk, pos, ks, rb, kp, ral, scaled2, upper2)
    return total(keep, across(give, 4))[None]


def solution(mesh):
    return jax.shard_map(
        eliminate,
        mesh=mesh,
        in_specs=(P("grid", "row", "col"), P(None, "grid", None, "col"), P(None, "grid", None)),
        out_specs=P("grid", "row", "col"),
        check_vma=False,
    )
```

time: 483 us -> 238 us (0.49)
  the two profiles are of different devices: /device:TPU:16 before, /device:TPU:1 now
where the time goes in v1:
time: 238 us; the launch traced here: 237 us
  starting transfers between devices  152 us (64%)
  waiting for transfers between devices  55.7 us (23%)
  Pallas kernels  19.8 us (8%)
  other arithmetic  4.53 us (2%)
  local copies, waits for them, and re-layouts  3.75 us (2%)
    ppermute x40, starting transfers between devices, move(): return lax.ppermute(block, axes, [(i, route(i)) for i in range(count)])  152 us
    ppermute x40, waiting for transfers between devices, move(): return lax.ppermute(block, axes, [(i, route(i)) for i in range(count)])  55.7 us
    pallas_call x3, Pallas kernels, scale(): call(body, (4,), [whole((rows, 256, 256))] * 4 + [pl.BlockSpec((1, 1024,...  8.69 us
  transfers between devices with their start and end apart: 40, of which 11 were waited for; matrix products, arithmetic and copies ran while one was open for 2% of the time, Pallas kernels for 7%

profile of v1, /device:TPU:1, one launch (start us, length us, event | category | flops | bytes accessed | tf_op | source)
XLA Modules:
  0.0 236.8 jit_solution(9956911864138272791)
XLA Ops:
  0.0 8.7 %collective-permute-start.6 = (bf16[3,4,256,256]{3,2,1,0:T(8,128)(2,1)}, bf16[3,4,256,256]{3,2,1,0:T(8,128)(2,1)S(1)}, u32[]{:S(2)}, u32[]{:S(2)}) collective-permute-start(bf16[3,4,256,256]{3,2,1,0:T(8,128)(2,1)} %bitcast.32), channel_id=1, source_target_pairs={{0,1},{1,0},{2,3},{3,2},{4,5},{5,4},{6,7},{7,6},{8,9},{9,8},{10,11... | collective-permute-start | bytes 4718600 | tf_op jit(solution)/shard_map/ppermute | solution.py:18
  15.4 7.7 %collective-permute-start.3 = (bf16[1,256,256]{2,1,0:T(8,128)(2,1)}, bf16[1,256,256]{2,1,0:T(8,128)(2,1)}, u32[]{:S(2)}, u32[]{:S(2)}) collective-permute-start(bf16[1,256,256]{2,1,0:T(8,128)(2,1)} %dynamic-slice_bitcast_fusion.1), channel_id=1, source_target_pairs={{0,2},{1,3},{2,0},{3,1},{4,6},{5,7},{6,4},{7,5},{8,10},{9,11},{10,... | collective-permute-start | bytes 393224 | tf_op jit(solution)/shard_map/ppermute | solution.py:18
  27.5 2.8 %collective-permute-start.4 = (bf16[1,256,256]{2,1,0:T(8,128)(2,1)}, bf16[1,256,256]{2,1,0:T(8,128)(2,1)S(1)}, u32[]{:S(2)}, u32[]{:S(2)}) collective-permute-start(bf16[1,256,256]{2,1,0:T(8,128)(2,1)} %collective-permute-done.3), channel_id=1, source_target_pairs={{0,4},{1,13},{2,6},{3,15},{4,0},{5,9},{6,2},{7,11},{8,12},{9,5},{1... | collective-permute-start | bytes 393224 | tf_op jit(solution)/shard_map/ppermute | solution.py:18
  37.8 9.1 %collective-permute-start = (bf16[3,256,256]{2,1,0:T(8,128)(2,1)S(1)}, bf16[3,256,256]{2,1,0:T(8,128)(2,1)S(1)}, u32[]{:S(2)}, u32[]{:S(2)}) collective-permute-start(bf16[3,256,256]{2,1,0:T(8,128)(2,1)S(1)} %copy-done.4), channel_id=1, source_target_pairs={{0,2},{1,3},{2,0},{3,1},{4,6},{5,7},{6,4},{7,5},{8,10},{9,11},{10,... | collective-permute-start | bytes 1179656 | tf_op jit(solution)/shard_map/ppermute | solution.py:18
  47.0 3.5 %collective-permute-start.17 = (bf16[2,256,256]{2,1,0:T(8,128)(2,1)S(1)}, bf16[2,256,256]{2,1,0:T(8,128)(2,1)S(1)}, u32[]{:S(2)}, u32[]{:S(2)}) collective-permute-start(bf16[2,256,256]{2,1,0:T(8,128)(2,1)S(1)} %collective-permute-done.16), channel_id=1, source_target_pairs={{0,4},{1,13},{2,6},{3,15},{4,0},{5,9},{6,2},{7,11},{8,12},{9,5},{1... | collective-permute-start | bytes 786440 | tf_op jit(solution)/shard_map/ppermute | solution.py:18
  51.5 3.4 %collective-permute-start.7 = (bf16[4,1,256,256]{3,2,1,0:T(8,128)(2,1)S(1)}, bf16[4,1,256,256]{3,2,1,0:T(8,128)(2,1)S(1)}, u32[]{:S(2)}, u32[]{:S(2)}) collective-permute-start(bf16[4,1,256,256]{3,2,1,0:T(8,128)(2,1)S(1)} %pad_maximum_fusion.2.dz), channel_id=1, source_target_pairs={{0,1},{1,0},{2,3},{3,2},{4,5},{5,4},{6,7},{7,6},{8,9},{9,8},{10,11... | collective-permute-start | bytes 1572872 | tf_op jit(solution)/shard_map/ppermute | solution.py:18
  55.0 4.0 %collective-permute-start.1 = (bf16[3,256,256]{2,1,0:T(8,128)(2,1)S(1)}, bf16[3,256,256]{2,1,0:T(8,128)(2,1)S(1)}, u32[]{:S(2)}, u32[]{:S(2)}) collective-permute-start(bf16[3,256,256]{2,1,0:T(8,128)(2,1)S(1)} %copy-done.4), channel_id=1, source_target_pairs={{0,1},{1,0},{2,3},{3,2},{4,5},{5,4},{6,7},{7,6},{8,9},{9,8},{10,11... | collective-permute-start | bytes 1179656 | tf_op jit(solution)/shard_map/ppermute | solution.py:18
  61.0 3.4 %collective-permute-start.18 = (bf16[2,2,256,256]{3,2,1,0:T(8,128)(2,1)S(1)}, bf16[2,2,256,256]{3,2,1,0:T(8,128)(2,1)S(1)}, u32[]{:S(2)}, u32[]{:S(2)}) collective-permute-start(bf16[2,2,256,256]{3,2,1,0:T(8,128)(2,1)S(1)} %pad_maximum_fusion.3), channel_id=1, source_target_pairs={{0,12},{1,5},{2,14},{3,7},{4,8},{5,1},{6,10},{7,3},{8,4},{9,13},{1... | collective-permute-start | bytes 1572872 | tf_op jit(solution)/shard_map/ppermute | solution.py:18
  67.0 3.6 %shard_map.39.s_ref = bf16[768,1024]{1,0:T(8,128)(2,1)S(1)} custom-call(s32[3,12]{1,0:T(4,128)S(1)} %bitcast.49, s32[3]{0:T(128)S(1)} %pad_add_fusion.pos_ref, bf16[3,256,256]{2,1,0:T(8,128)(2,1)S(1)} %copy-done.4, bf16[3,256,256]{2,1,0:T(8,128)(2,1)S(1)} %collective-permute-done.l1, bf16[3,256,256]{2,1,0:T(8,128)(2,1)S(1)} %collective-permute-done.1.l2, ...), custom_call_target="tpu_custom_call" | custom-call | flops 1610612736 | bytes 4194304 | tf_op jit(solution)/shard_map/pallas_call | solution.py:199
  73.0 12.3 %collective-permute-start.20 = (bf16[3,128,256]{2,1,0:T(8,128)(2,1)S(1)}, bf16[3,128,256]{2,1,0:T(8,128)(2,1)S(1)}, u32[]{:S(2)}, u32[]{:S(2)}) collective-permute-start(bf16[3,128,256]{2,1,0:T(8,128)(2,1)S(1)} %get-tuple-element.29), channel_id=1, source_target_pairs={{0,16},{16,0},{32,48},{48,32},{64,80},{80,64},{96,112},{112,96},{1... | collective-permute-start | bytes 589832 | tf_op jit(solution)/shard_map/ppermute | solution.py:18
  85.4 3.1 %collective-permute-start.19 = (bf16[4,2,256,256]{3,2,1,0:T(8,128)(2,1)S(1)}, bf16[4,2,256,256]{3,2,1,0:T(8,128)(2,1)S(1)}, u32[]{:S(2)}, u32[]{:S(2)}) collective-permute-start(bf16[4,2,256,256]{3,2,1,0:T(8,128)(2,1)S(1)} %pad_maximum_fusion.dz), channel_id=1, source_target_pairs={{0,1},{1,0},{2,3},{3,2},{4,5},{5,4},{6,7},{7,6},{8,9},{9,8},{10,11... | collective-permute-start | bytes 3145736 | tf_op jit(solution)/shard_map/ppermute | solution.py:18
  90.4 3.4 %collective-permute-start.23 = (bf16[3,128,256]{2,1,0:T(8,128)(2,1)S(1)}, bf16[3,128,256]{2,1,0:T(8,128)(2,1)S(1)}, u32[]{:S(2)}, u32[]{:S(2)}) collective-permute-start(bf16[3,128,256]{2,1,0:T(8,128)(2,1)S(1)} %get-tuple-element.30), channel_id=1, source_target_pairs={{0,16},{16,0},{32,48},{48,32},{64,80},{80,64},{96,112},{112,96},{1... | collective-permute-start | bytes 589832 | tf_op jit(solution)/shard_map/ppermute | solution.py:18
  96.3 6.2 %collective-permute-done.23 = bf16[3,128,256]{2,1,0:T(8,128)(2,1)S(1)} collective-permute-done((bf16[3,128,256]{2,1,0:T(8,128)(2,1)S(1)}, bf16[3,128,256]{2,1,0:T(8,128)(2,1)S(1)}, u32[]{:S(2)}, u32[]{:S(2)}) %collective-permute-start.23) | collective-permute-done | bytes 196640 | tf_op jit(solution)/shard_map/ppermute | solution.py:18
  105.0 7.3 %collective-permute-start.13 = (bf16[2,256,256]{2,1,0:T(8,128)(2,1)S(1)}, bf16[2,256,256]{2,1,0:T(8,128)(2,1)S(1)}, u32[]{:S(2)}, u32[]{:S(2)}) collective-permute-start(bf16[2,256,256]{2,1,0:T(8,128)(2,1)S(1)} %add_convert_fusion.1.l0), channel_id=1, source_target_pairs={{0,2},{1,3},{2,0},{3,1},{4,6},{5,7},{6,4},{7,5},{8,10},{9,11},{10,... | collective-permute-start | bytes 786440 | tf_op jit(solution)/shard_map/ppermute | solution.py:18
  112.3 2.9 %collective-permute-start.14 = (bf16[2,256,256]{2,1,0:T(8,128)(2,1)S(1)}, bf16[2,256,256]{2,1,0:T(8,128)(2,1)S(1)}, u32[]{:S(2)}, u32[]{:S(2)}) collective-permute-start(bf16[2,256,256]{2,1,0:T(8,128)(2,1)S(1)} %add_convert_fusion.1.l0), channel_id=1, source_target_pairs={{0,1},{1,0},{2,3},{3,2},{4,5},{5,4},{6,7},{7,6},{8,9},{9,8},{10,11... | collective-permute-start | bytes 786440 | tf_op jit(solution)/shard_map/ppermute | solution.py:18
  117.3 3.6 %collective-permute-start.22 = (bf16[2,3,128,256]{3,2,1,0:T(8,128)(2,1)S(1)}, bf16[2,3,128,256]{3,2,1,0:T(8,128)(2,1)S(1)}, u32[]{:S(2)}, u32[]{:S(2)}) collective-permute-start(bf16[2,3,128,256]{3,2,1,0:T(8,128)(2,1)S(1)} %pad_maximum_fusion.4), channel_id=1, source_target_pairs={{0,12},{1,5},{2,14},{3,7},{4,8},{5,1},{6,10},{7,3},{8,4},{9,13},{1... | collective-permute-start | bytes 1179656 | tf_op jit(solution)/shard_map/ppermute | solution.py:18
  121.0 6.8 %collective-permute-start.25 = (bf16[2,3,128,256]{3,2,1,0:T(8,128)(2,1)S(1)}, bf16[2,3,128,256]{3,2,1,0:T(8,128)(2,1)S(1)}, u32[]{:S(2)}, u32[]{:S(2)}) collective-permute-start(bf16[2,3,128,256]{3,2,1,0:T(8,128)(2,1)S(1)} %pad_maximum_fusion.5), channel_id=1, source_target_pairs={{0,12},{1,5},{2,14},{3,7},{4,8},{5,1},{6,10},{7,3},{8,4},{9,13},{1... | collective-permute-start | bytes 1179656 | tf_op jit(solution)/shard_map/ppermute | solution.py:18
  127.8 2.8 %collective-permute-start.11 = (bf16[3,256,256]{2,1,0:T(8,128)(2,1)S(1)}, bf16[3,256,256]{2,1,0:T(8,128)(2,1)S(1)}, u32[]{:S(2)}, u32[]{:S(2)}) collective-permute-start(bf16[3,256,256]{2,1,0:T(8,128)(2,1)S(1)} %get-tuple-element.26), channel_id=1, source_target_pairs={{0,16},{16,0},{32,48},{48,32},{64,80},{80,64},{96,112},{112,96},{1... | collective-permute-start | bytes 1179656 | tf_op jit(solution)/shard_map/ppermute | solution.py:18
  130.7 4.4 %collective-permute-start.15 = (bf16[2,256,256]{2,1,0:T(8,128)(2,1)S(1)}, bf16[2,256,256]{2,1,0:T(8,128)(2,1)S(1)}, u32[]{:S(2)}, u32[]{:S(2)}) collective-permute-start(bf16[2,256,256]{2,1,0:T(8,128)(2,1)S(1)} %collective-permute-done.13.l1), channel_id=1, source_target_pairs={{0,1},{1,0},{2,3},{3,2},{4,5},{5,4},{6,7},{7,6},{8,9},{9,8},{10,11... | collective-permute-start | bytes 786440 | tf_op jit(solution)/shard_map/ppermute | solution.py:18
  136.3 2.9 %shard_map.43.s_ref = bf16[512,1024]{1,0:T(8,128)(2,1)S(1)} custom-call(s32[3,12]{1,0:T(4,128)S(1)} %bitcast.52, s32[3]{0:T(128)S(1)} %pad_add_fusion.pos_ref, bf16[2,256,256]{2,1,0:T(8,128)(2,1)S(1)} %add_convert_fusion.1.l0, bf16[2,256,256]{2,1,0:T(8,128)(2,1)S(1)} %collective-permute-done.13.l1, bf16[2,256,256]{2,1,0:T(8,128)(2,1)S(1)} %collective-permute-done.14.l2, ...), custom_call_target="tpu_custom_call" | custom-call | flops 1073741824 | bytes 4194304 | tf_op jit(solution)/shard_map/pallas_call | solution.py:199
  141.0 4.2 %collective-permute-start.31 = (bf16[3,128,256]{2,1,0:T(8,128)(2,1)S(1)}, bf16[3,128,256]{2,1,0:T(8,128)(2,1)S(1)}, u32[]{:S(2)}, u32[]{:S(2)}) collective-permute-start(bf16[3,128,256]{2,1,0:T(8,128)(2,1)S(1)} %get-tuple-element.35), channel_id=1, source_target_pairs={{0,32},{16,48},{32,0},{48,16},{64,96},{80,112},{96,64},{112,80},{1... | collective-permute-start | bytes 589832 | tf_op jit(solution)/shard_map/ppermute | solution.py:18
  147.2 10.1 %collective-permute-done.31 = bf16[3,128,256]{2,1,0:T(8,128)(2,1)S(1)} collective-permute-done((bf16[3,128,256]{2,1,0:T(8,128)(2,1)S(1)}, bf16[3,128,256]{2,1,0:T(8,128)(2,1)S(1)}, u32[]{:S(2)}, u32[]{:S(2)}) %collective-permute-start.31) | collective-permute-done | bytes 196640 | tf_op jit(solution)/shard_map/ppermute | solution.py:18
  165.2 7.0 %collective-permute-start.33 = (bf16[3,128,256]{2,1,0:T(8,128)(2,1)S(1)}, bf16[3,128,256]{2,1,0:T(8,128)(2,1)S(1)}, u32[]{:S(2)}, u32[]{:S(2)}) collective-permute-start(bf16[3,128,256]{2,1,0:T(8,128)(2,1)S(1)} %add_convert_fusion.4.refs_0_), channel_id=1, source_target_pairs={{0,4},{1,13},{2,6},{3,15},{4,0},{5,9},{6,2},{7,11},{8,12},{9,5},{1... | collective-permute-start | bytes 589832 | tf_op jit(solution)/shard_map/ppermute | solution.py:18
  172.3 4.2 %collective-permute-start.37 = (bf16[3,128,256]{2,1,0:T(8,128)(2,1)S(1)}, bf16[3,128,256]{2,1,0:T(8,128)(2,1)S(1)}, u32[]{:S(2)}, u32[]{:S(2)}) collective-permute-start(bf16[3,128,256]{2,1,0:T(8,128)(2,1)S(1)} %add_convert_fusion.2.refs_3_), channel_id=1, source_target_pairs={{0,4},{1,13},{2,6},{3,15},{4,0},{5,9},{6,2},{7,11},{8,12},{9,5},{1... | collective-permute-start | bytes 589832 | tf_op jit(solution)/shard_map/ppermute | solution.py:18
  178.5 4.3 %collective-permute-start.27 = (bf16[1,256,256]{2,1,0:T(8,128)(2,1)S(1)}, bf16[1,256,256]{2,1,0:T(8,128)(2,1)S(1)}, u32[]{:S(2)}, u32[]{:S(2)}) collective-permute-start(bf16[1,256,256]{2,1,0:T(8,128)(2,1)S(1)} %get-tuple-element.34), channel_id=1, source_target_pairs={{0,32},{16,48},{32,0},{48,16},{64,96},{80,112},{96,64},{112,80},{1... | collective-permute-start | bytes 393224 | tf_op jit(solution)/shard_map/ppermute | solution.py:18
  184.8 3.4 %collective-permute-start.38 = (bf16[2,3,128,256]{3,2,1,0:T(8,128)(2,1)S(1)}, bf16[2,3,128,256]{3,2,1,0:T(8,128)(2,1)S(1)}, u32[]{:S(2)}, u32[]{:S(2)}) collective-permute-start(bf16[2,3,128,256]{3,2,1,0:T(8,128)(2,1)S(1)} %pad_maximum_fusion.7), channel_id=1, source_target_pairs={{0,12},{1,5},{2,14},{3,7},{4,8},{5,1},{6,10},{7,3},{8,4},{9,13},{1... | collective-permute-start | bytes 1179656 | tf_op jit(solution)/shard_map/ppermute | solution.py:18
  188.2 16.3 %collective-permute-done.27.ra_ref = bf16[1,256,256]{2,1,0:T(8,128)(2,1)S(1)} collective-permute-done((bf16[1,256,256]{2,1,0:T(8,128)(2,1)S(1)}, bf16[1,256,256]{2,1,0:T(8,128)(2,1)S(1)}, u32[]{:S(2)}, u32[]{:S(2)}) %collective-permute-start.27) | collective-permute-done | bytes 131104 | tf_op jit(solution)/shard_map/ppermute | solution.py:18
  204.5 4.6 %collective-permute-start.28 = (bf16[1,256,256]{2,1,0:T(8,128)(2,1)S(1)}, bf16[1,256,256]{2,1,0:T(8,128)(2,1)S(1)}, u32[]{:S(2)}, u32[]{:S(2)}) collective-permute-start(bf16[1,256,256]{2,1,0:T(8,128)(2,1)S(1)} %add_convert_fusion.8.l0), channel_id=1, source_target_pairs={{0,2},{1,3},{2,0},{3,1},{4,6},{5,7},{6,4},{7,5},{8,10},{9,11},{10,... | collective-permute-start | bytes 393224 | tf_op jit(solution)/shard_map/ppermute | solution.py:18
  209.1 2.7 %collective-permute-start.29 = (bf16[1,256,256]{2,1,0:T(8,128)(2,1)S(1)}, bf16[1,256,256]{2,1,0:T(8,128)(2,1)S(1)}, u32[]{:S(2)}, u32[]{:S(2)}) collective-permute-start(bf16[1,256,256]{2,1,0:T(8,128)(2,1)S(1)} %add_convert_fusion.8.l0), channel_id=1, source_target_pairs={{0,1},{1,0},{2,3},{3,2},{4,5},{5,4},{6,7},{7,6},{8,9},{9,8},{10,11... | collective-permute-start | bytes 393224 | tf_op jit(solution)/shard_map/ppermute | solution.py:18
  211.8 6.3 %collective-permute-done.28.l1 = bf16[1,256,256]{2,1,0:T(8,128)(2,1)S(1)} collective-permute-done((bf16[1,256,256]{2,1,0:T(8,128)(2,1)S(1)}, bf16[1,256,256]{2,1,0:T(8,128)(2,1)S(1)}, u32[]{:S(2)}, u32[]{:S(2)}) %collective-permute-start.28) | collective-permute-done | bytes 131104 | tf_op jit(solution)/shard_map/ppermute | solution.py:18
  218.1 2.4 %collective-permute-start.30 = (bf16[1,256,256]{2,1,0:T(8,128)(2,1)S(1)}, bf16[1,256,256]{2,1,0:T(8,128)(2,1)S(1)}, u32[]{:S(2)}, u32[]{:S(2)}) collective-permute-start(bf16[1,256,256]{2,1,0:T(8,128)(2,1)S(1)} %collective-permute-done.28.l1), channel_id=1, source_target_pairs={{0,1},{1,0},{2,3},{3,2},{4,5},{5,4},{6,7},{7,6},{8,9},{9,8},{10,11... | collective-permute-start | bytes 393224 | tf_op jit(solution)/shard_map/ppermute | solution.py:18
  228.0 8.0 %collective-permute-done.39 = bf16[128,1024]{1,0:T(8,128)(2,1)S(1)} collective-permute-done((bf16[128,1024]{1,0:T(8,128)(2,1)S(1)}, bf16[128,1024]{1,0:T(8,128)(2,1)S(1)}, u32[]{:S(2)}, u32[]{:S(2)}) %collective-permute-start.39) | collective-permute-done | bytes 262176 | tf_op jit(solution)/shard_map/ppermute | solution.py:18
  (92 shorter events, 60.3 us)
Async XLA Ops:
  0.0 66.1 %collective-permute-start.6 = (bf16[3,4,256,256]{3,2,1,0:T(8,128)(2,1)}, bf16[3,4,256,256]{3,2,1,0:T(8,128)(2,1)S(1)}, u32[]{:S(2)}, u32[]{:S(2)}) collective-permute-start(bf16[3,4,256,256]{3,2,1,0:T(8,128)(2,1)} %bitcast.32), channel_id=1, source_target_pairs={{0,1},{1,0},{2,3},{3,2},{4,5},{5,4},{6,7},{7,6},{8,9},{9,8},{10,11... | collective-permute-start | bytes 4718600 | tf_op jit(solution)/shard_map/ppermute | solution.py:18
  12.8 17.4 %collective-permute-start.8 = (bf16[3,256,256]{2,1,0:T(8,128)(2,1)S(1)}, bf16[3,256,256]{2,1,0:T(8,128)(2,1)}, u32[]{:S(2)}, u32[]{:S(2)}) collective-permute-start(bf16[3,256,256]{2,1,0:T(8,128)(2,1)S(1)} %get-tuple-element.23.refs_0_), channel_id=1, source_target_pairs={{0,4},{1,13},{2,6},{3,15},{4,0},{5,9},{6,2},{7,11},{8,12},{9,5},{1... | collective-permute-start | bytes 1179656 | tf_op jit(solution)/shard_map/ppermute | solution.py:18
  15.4 12.1 %collective-permute-start.3 = (bf16[1,256,256]{2,1,0:T(8,128)(2,1)}, bf16[1,256,256]{2,1,0:T(8,128)(2,1)}, u32[]{:S(2)}, u32[]{:S(2)}) collective-permute-start(bf16[1,256,256]{2,1,0:T(8,128)(2,1)} %dynamic-slice_bitcast_fusion.1), channel_id=1, source_target_pairs={{0,2},{1,3},{2,0},{3,1},{4,6},{5,7},{6,4},{7,5},{8,10},{9,11},{10,... | collective-permute-start | bytes 393224 | tf_op jit(solution)/shard_map/ppermute | solution.py:18
  23.2 23.7 %collective-permute-start.16 = (bf16[2,256,256]{2,1,0:T(8,128)(2,1)S(1)}, bf16[2,256,256]{2,1,0:T(8,128)(2,1)S(1)}, u32[]{:S(2)}, u32[]{:S(2)}) collective-permute-start(bf16[2,256,256]{2,1,0:T(8,128)(2,1)S(1)} %dynamic-slice_bitcast_fusion), channel_id=1, source_target_pairs={{0,2},{1,3},{2,0},{3,1},{4,6},{5,7},{6,4},{7,5},{8,10},{9,11},{10,... | collective-permute-start | bytes 786440 | tf_op jit(solution)/shard_map/ppermute | solution.py:18
  31.4 29.6 %collective-permute-start.9 = (bf16[2,3,256,256]{3,2,1,0:T(8,128)(2,1)S(1)}, bf16[2,3,256,256]{3,2,1,0:T(8,128)(2,1)S(1)}, u32[]{:S(2)}, u32[]{:S(2)}) collective-permute-start(bf16[2,3,256,256]{3,2,1,0:T(8,128)(2,1)S(1)} %pad_maximum_fusion.1), channel_id=1, source_target_pairs={{0,12},{1,5},{2,14},{3,7},{4,8},{5,1},{6,10},{7,3},{8,4},{9,13},{1... | collective-permute-start | bytes 2359304 | tf_op jit(solution)/shard_map/ppermute | solution.py:18
  35.9 14.6 %collective-permute-start.5 = (bf16[2,1,256,256]{3,2,1,0:T(8,128)(2,1)S(1)}, bf16[2,1,256,256]{3,2,1,0:T(8,128)(2,1)S(1)}, u32[]{:S(2)}, u32[]{:S(2)}) collective-permute-start(bf16[2,1,256,256]{3,2,1,0:T(8,128)(2,1)S(1)} %pad_maximum_fusion.8), channel_id=1, source_target_pairs={{0,12},{1,5},{2,14},{3,7},{4,8},{5,1},{6,10},{7,3},{8,4},{9,13},{1... | collective-permute-start | bytes 786440 | tf_op jit(solution)/shard_map/ppermute | solution.py:18
  37.8 17.2 %collective-permute-start = (bf16[3,256,256]{2,1,0:T(8,128)(2,1)S(1)}, bf16[3,256,256]{2,1,0:T(8,128)(2,1)S(1)}, u32[]{:S(2)}, u32[]{:S(2)}) collective-permute-start(bf16[3,256,256]{2,1,0:T(8,128)(2,1)S(1)} %copy-done.4), channel_id=1, source_target_pairs={{0,2},{1,3},{2,0},{3,1},{4,6},{5,7},{6,4},{7,5},{8,10},{9,11},{10,... | collective-permute-start | bytes 1179656 | tf_op jit(solution)/shard_map/ppermute | solution.py:18
  47.0 12.1 %collective-permute-start.17 = (bf16[2,256,256]{2,1,0:T(8,128)(2,1)S(1)}, bf16[2,256,256]{2,1,0:T(8,128)(2,1)S(1)}, u32[]{:S(2)}, u32[]{:S(2)}) collective-permute-start(bf16[2,256,256]{2,1,0:T(8,128)(2,1)S(1)} %collective-permute-done.16), channel_id=1, source_target_pairs={{0,4},{1,13},{2,6},{3,15},{4,0},{5,9},{6,2},{7,11},{8,12},{9,5},{1... | collective-permute-start | bytes 786440 | tf_op jit(solution)/shard_map/ppermute | solution.py:18
  51.5 14.6 %collective-permute-start.7 = (bf16[4,1,256,256]{3,2,1,0:T(8,128)(2,1)S(1)}, bf16[4,1,256,256]{3,2,1,0:T(8,128)(2,1)S(1)}, u32[]{:S(2)}, u32[]{:S(2)}) collective-permute-start(bf16[4,1,256,256]{3,2,1,0:T(8,128)(2,1)S(1)} %pad_maximum_fusion.2.dz), channel_id=1, source_target_pairs={{0,1},{1,0},{2,3},{3,2},{4,5},{5,4},{6,7},{7,6},{8,9},{9,8},{10,11... | collective-permute-start | bytes 1572872 | tf_op jit(solution)/shard_map/ppermute | solution.py:18
  55.0 12.0 %collective-permute-start.1 = (bf16[3,256,256]{2,1,0:T(8,128)(2,1)S(1)}, bf16[3,256,256]{2,1,0:T(8,128)(2,1)S(1)}, u32[]{:S(2)}, u32[]{:S(2)}) collective-permute-start(bf16[3,256,256]{2,1,0:T(8,128)(2,1)S(1)} %copy-done.4), channel_id=1, source_target_pairs={{0,1},{1,0},{2,3},{3,2},{4,5},{5,4},{6,7},{7,6},{8,9},{9,8},{10,11... | collective-permute-start | bytes 1179656 | tf_op jit(solution)/shard_map/ppermute | solution.py:18
  61.0 24.3 %collective-permute-start.18 = (bf16[2,2,256,256]{3,2,1,0:T(8,128)(2,1)S(1)}, bf16[2,2,256,256]{3,2,1,0:T(8,128)(2,1)S(1)}, u32[]{:S(2)}, u32[]{:S(2)}) collective-permute-start(bf16[2,2,256,256]{3,2,1,0:T(8,128)(2,1)S(1)} %pad_maximum_fusion.3), channel_id=1, source_target_pairs={{0,12},{1,5},{2,14},{3,7},{4,8},{5,1},{6,10},{7,3},{8,4},{9,13},{1... | collective-permute-start | bytes 1572872 | tf_op jit(solution)/shard_map/ppermute | solution.py:18
  73.0 20.9 %collective-permute-start.20 = (bf16[3,128,256]{2,1,0:T(8,128)(2,1)S(1)}, bf16[3,128,256]{2,1,0:T(8,128)(2,1)S(1)}, u32[]{:S(2)}, u32[]{:S(2)}) collective-permute-start(bf16[3,128,256]{2,1,0:T(8,128)(2,1)S(1)} %get-tuple-element.29), channel_id=1, source_target_pairs={{0,16},{16,0},{32,48},{48,32},{64,80},{80,64},{96,112},{112,96},{1... | collective-permute-start | bytes 589832 | tf_op jit(solution)/shard_map/ppermute | solution.py:18
  85.4 45.3 %collective-permute-start.19 = (bf16[4,2,256,256]{3,2,1,0:T(8,128)(2,1)S(1)}, bf16[4,2,256,256]{3,2,1,0:T(8,128)(2,1)S(1)}, u32[]{:S(2)}, u32[]{:S(2)}) collective-permute-start(bf16[4,2,256,256]{3,2,1,0:T(8,128)(2,1)S(1)} %pad_maximum_fusion.dz), channel_id=1, source_target_pairs={{0,1},{1,0},{2,3},{3,2},{4,5},{5,4},{6,7},{7,6},{8,9},{9,8},{10,11... | collective-permute-start | bytes 3145736 | tf_op jit(solution)/shard_map/ppermute | solution.py:18
  88.5 16.4 %collective-permute-start.12 = (bf16[2,256,256]{2,1,0:T(8,128)(2,1)S(1)}, bf16[2,256,256]{2,1,0:T(8,128)(2,1)S(1)}, u32[]{:S(2)}, u32[]{:S(2)}) collective-permute-start(bf16[2,256,256]{2,1,0:T(8,128)(2,1)S(1)} %get-tuple-element.28), channel_id=1, source_target_pairs={{0,16},{16,0},{32,48},{48,32},{64,80},{80,64},{96,112},{112,96},{1... | collective-permute-start | bytes 786440 | tf_op jit(solution)/shard_map/ppermute | solution.py:18
  90.4 12.0 %collective-permute-start.23 = (bf16[3,128,256]{2,1,0:T(8,128)(2,1)S(1)}, bf16[3,128,256]{2,1,0:T(8,128)(2,1)S(1)}, u32[]{:S(2)}, u32[]{:S(2)}) collective-permute-start(bf16[3,128,256]{2,1,0:T(8,128)(2,1)S(1)} %get-tuple-element.30), channel_id=1, source_target_pairs={{0,16},{16,0},{32,48},{48,32},{64,80},{80,64},{96,112},{112,96},{1... | collective-permute-start | bytes 589832 | tf_op jit(solution)/shard_map/ppermute | solution.py:18
  93.9 21.4 %collective-permute-start.21 = (bf16[3,128,256]{2,1,0:T(8,128)(2,1)S(1)}, bf16[3,128,256]{2,1,0:T(8,128)(2,1)S(1)}, u32[]{:S(2)}, u32[]{:S(2)}) collective-permute-start(bf16[3,128,256]{2,1,0:T(8,128)(2,1)S(1)} %add_convert_fusion.7.refs_0_), channel_id=1, source_target_pairs={{0,4},{1,13},{2,6},{3,15},{4,0},{5,9},{6,2},{7,11},{8,12},{9,5},{1... | collective-permute-start | bytes 589832 | tf_op jit(solution)/shard_map/ppermute | solution.py:18
  102.5 14.7 %collective-permute-start.24 = (bf16[3,128,256]{2,1,0:T(8,128)(2,1)S(1)}, bf16[3,128,256]{2,1,0:T(8,128)(2,1)S(1)}, u32[]{:S(2)}, u32[]{:S(2)}) collective-permute-start(bf16[3,128,256]{2,1,0:T(8,128)(2,1)S(1)} %add_convert_fusion.6.refs_3_), channel_id=1, source_target_pairs={{0,4},{1,13},{2,6},{3,15},{4,0},{5,9},{6,2},{7,11},{8,12},{9,5},{1... | collective-permute-start | bytes 589832 | tf_op jit(solution)/shard_map/ppermute | solution.py:18
  105.0 16.0 %collective-permute-start.13 = (bf16[2,256,256]{2,1,0:T(8,128)(2,1)S(1)}, bf16[2,256,256]{2,1,0:T(8,128)(2,1)S(1)}, u32[]{:S(2)}, u32[]{:S(2)}) collective-permute-start(bf16[2,256,256]{2,1,0:T(8,128)(2,1)S(1)} %add_convert_fusion.1.l0), channel_id=1, source_target_pairs={{0,2},{1,3},{2,0},{3,1},{4,6},{5,7},{6,4},{7,5},{8,10},{9,11},{10,... | collective-permute-start | bytes 786440 | tf_op jit(solution)/shard_map/ppermute | solution.py:18
  112.3 15.5 %collective-permute-start.14 = (bf16[2,256,256]{2,1,0:T(8,128)(2,1)S(1)}, bf16[2,256,256]{2,1,0:T(8,128)(2,1)S(1)}, u32[]{:S(2)}, u32[]{:S(2)}) collective-permute-start(bf16[2,256,256]{2,1,0:T(8,128)(2,1)S(1)} %add_convert_fusion.1.l0), channel_id=1, source_target_pairs={{0,1},{1,0},{2,3},{3,2},{4,5},{5,4},{6,7},{7,6},{8,9},{9,8},{10,11... | collective-permute-start | bytes 786440 | tf_op jit(solution)/shard_map/ppermute | solution.py:18
  115.3 24.7 %collective-permute-start.10 = (bf16[3,256,256]{2,1,0:T(8,128)(2,1)S(1)}, bf16[3,256,256]{2,1,0:T(8,128)(2,1)S(1)}, u32[]{:S(2)}, u32[]{:S(2)}) collective-permute-start(bf16[3,256,256]{2,1,0:T(8,128)(2,1)S(1)} %get-tuple-element.25), channel_id=1, source_target_pairs={{0,16},{16,0},{32,48},{48,32},{64,80},{80,64},{96,112},{112,96},{1... | collective-permute-start | bytes 1179656 | tf_op jit(solution)/shard_map/ppermute | solution.py:18
  117.3 22.0 %collective-permute-start.22 = (bf16[2,3,128,256]{3,2,1,0:T(8,128)(2,1)S(1)}, bf16[2,3,128,256]{3,2,1,0:T(8,128)(2,1)S(1)}, u32[]{:S(2)}, u32[]{:S(2)}) collective-permute-start(bf16[2,3,128,256]{3,2,1,0:T(8,128)(2,1)S(1)} %pad_maximum_fusion.4), channel_id=1, source_target_pairs={{0,12},{1,5},{2,14},{3,7},{4,8},{5,1},{6,10},{7,3},{8,4},{9,13},{1... | collective-permute-start | bytes 1179656 | tf_op jit(solution)/shard_map/ppermute | solution.py:18
  121.0 18.3 %collective-permute-start.25 = (bf16[2,3,128,256]{3,2,1,0:T(8,128)(2,1)S(1)}, bf16[2,3,128,256]{3,2,1,0:T(8,128)(2,1)S(1)}, u32[]{:S(2)}, u32[]{:S(2)}) collective-permute-start(bf16[2,3,128,256]{3,2,1,0:T(8,128)(2,1)S(1)} %pad_maximum_fusion.5), channel_id=1, source_target_pairs={{0,12},{1,5},{2,14},{3,7},{4,8},{5,1},{6,10},{7,3},{8,4},{9,13},{1... | collective-permute-start | bytes 1179656 | tf_op jit(solution)/shard_map/ppermute | solution.py:18
  127.8 12.1 %collective-permute-start.11 = (bf16[3,256,256]{2,1,0:T(8,128)(2,1)S(1)}, bf16[3,256,256]{2,1,0:T(8,128)(2,1)S(1)}, u32[]{:S(2)}, u32[]{:S(2)}) collective-permute-start(bf16[3,256,256]{2,1,0:T(8,128)(2,1)S(1)} %get-tuple-element.26), channel_id=1, source_target_pairs={{0,16},{16,0},{32,48},{48,32},{64,80},{80,64},{96,112},{112,96},{1... | collective-permute-start | bytes 1179656 | tf_op jit(solution)/shard_map/ppermute | solution.py:18
  141.0 16.3 %collective-permute-start.31 = (bf16[3,128,256]{2,1,0:T(8,128)(2,1)S(1)}, bf16[3,128,256]{2,1,0:T(8,128)(2,1)S(1)}, u32[]{:S(2)}, u32[]{:S(2)}) collective-permute-start(bf16[3,128,256]{2,1,0:T(8,128)(2,1)S(1)} %get-tuple-element.35), channel_id=1, source_target_pairs={{0,32},{16,48},{32,0},{48,16},{64,96},{80,112},{96,64},{112,80},{1... | collective-permute-start | bytes 589832 | tf_op jit(solution)/shard_map/ppermute | solution.py:18
  145.2 16.4 %collective-permute-start.35 = (bf16[3,128,256]{2,1,0:T(8,128)(2,1)S(1)}, bf16[3,128,256]{2,1,0:T(8,128)(2,1)S(1)}, u32[]{:S(2)}, u32[]{:S(2)}) collective-permute-start(bf16[3,128,256]{2,1,0:T(8,128)(2,1)S(1)} %get-tuple-element.36), channel_id=1, source_target_pairs={{0,32},{16,48},{32,0},{48,16},{64,96},{80,112},{96,64},{112,80},{1... | collective-permute-start | bytes 589832 | tf_op jit(solution)/shard_map/ppermute | solution.py:18
  165.2 17.5 %collective-permute-start.33 = (bf16[3,128,256]{2,1,0:T(8,128)(2,1)S(1)}, bf16[3,128,256]{2,1,0:T(8,128)(2,1)S(1)}, u32[]{:S(2)}, u32[]{:S(2)}) collective-permute-start(bf16[3,128,256]{2,1,0:T(8,128)(2,1)S(1)} %add_convert_fusion.4.refs_0_), channel_id=1, source_target_pairs={{0,4},{1,13},{2,6},{3,15},{4,0},{5,9},{6,2},{7,11},{8,12},{9,5},{1... | collective-permute-start | bytes 589832 | tf_op jit(solution)/shard_map/ppermute | solution.py:18
  172.3 12.4 %collective-permute-start.37 = (bf16[3,128,256]{2,1,0:T(8,128)(2,1)S(1)}, bf16[3,128,256]{2,1,0:T(8,128)(2,1)S(1)}, u32[]{:S(2)}, u32[]{:S(2)}) collective-permute-start(bf16[3,128,256]{2,1,0:T(8,128)(2,1)S(1)} %add_convert_fusion.2.refs_3_), channel_id=1, source_target_pairs={{0,4},{1,13},{2,6},{3,15},{4,0},{5,9},{6,2},{7,11},{8,12},{9,5},{1... | collective-permute-start | bytes 589832 | tf_op jit(solution)/shard_map/ppermute | solution.py:18
  176.6 47.9 %collective-permute-start.26 = (bf16[3,256,256]{2,1,0:T(8,128)(2,1)S(1)}, bf16[3,256,256]{2,1,0:T(8,128)(2,1)S(1)}, u32[]{:S(2)}, u32[]{:S(2)}) collective-permute-start(bf16[3,256,256]{2,1,0:T(8,128)(2,1)S(1)} %get-tuple-element.32), channel_id=1, source_target_pairs={{0,32},{16,48},{32,0},{48,16},{64,96},{80,112},{96,64},{112,80},{1... | collective-permute-start | bytes 1179656 | tf_op jit(solution)/shard_map/ppermute | solution.py:18
  178.5 25.9 %collective-permute-start.27 = (bf16[1,256,256]{2,1,0:T(8,128)(2,1)S(1)}, bf16[1,256,256]{2,1,0:T(8,128)(2,1)S(1)}, u32[]{:S(2)}, u32[]{:S(2)}) collective-permute-start(bf16[1,256,256]{2,1,0:T(8,128)(2,1)S(1)} %get-tuple-element.34), channel_id=1, source_target_pairs={{0,32},{16,48},{32,0},{48,16},{64,96},{80,112},{96,64},{112,80},{1... | collective-permute-start | bytes 393224 | tf_op jit(solution)/shard_map/ppermute | solution.py:18
  182.8 40.9 %collective-permute-start.34 = (bf16[2,3,128,256]{3,2,1,0:T(8,128)(2,1)S(1)}, bf16[2,3,128,256]{3,2,1,0:T(8,128)(2,1)S(1)}, u32[]{:S(2)}, u32[]{:S(2)}) collective-permute-start(bf16[2,3,128,256]{3,2,1,0:T(8,128)(2,1)S(1)} %pad_maximum_fusion.6), channel_id=1, source_target_pairs={{0,12},{1,5},{2,14},{3,7},{4,8},{5,1},{6,10},{7,3},{8,4},{9,13},{1... | collective-permute-start | bytes 1179656 | tf_op jit(solution)/shard_map/ppermute | solution.py:18
  184.8 39.0 %collective-permute-start.38 = (bf16[2,3,128,256]{3,2,1,0:T(8,128)(2,1)S(1)}, bf16[2,3,128,256]{3,2,1,0:T(8,128)(2,1)S(1)}, u32[]{:S(2)}, u32[]{:S(2)}) collective-permute-start(bf16[2,3,128,256]{3,2,1,0:T(8,128)(2,1)S(1)} %pad_maximum_fusion.7), channel_id=1, source_target_pairs={{0,12},{1,5},{2,14},{3,7},{4,8},{5,1},{6,10},{7,3},{8,4},{9,13},{1... | collective-permute-start | bytes 1179656 | tf_op jit(solution)/shard_map/ppermute | solution.py:18
  204.5 13.7 %collective-permute-start.28 = (bf16[1,256,256]{2,1,0:T(8,128)(2,1)S(1)}, bf16[1,256,256]{2,1,0:T(8,128)(2,1)S(1)}, u32[]{:S(2)}, u32[]{:S(2)}) collective-permute-start(bf16[1,256,256]{2,1,0:T(8,128)(2,1)S(1)} %add_convert_fusion.8.l0), channel_id=1, source_target_pairs={{0,2},{1,3},{2,0},{3,1},{4,6},{5,7},{6,4},{7,5},{8,10},{9,11},{10,... | collective-permute-start | bytes 393224 | tf_op jit(solution)/shard_map/ppermute | solution.py:18
  (13 other events, 88.4 us)

commit v2 on v1

--- a/solution.py
+++ b/solution.py
@@ -86,7 +86,7 @@
         ),
         out_shape=out_shape,
         compiler_params=pltpu.CompilerParams(
-            dimension_semantics=("arbitrary",) * len(grid), vmem_limit_bytes=32 * 2**20
+            dimension_semantics=("arbitrary",) * len(grid), vmem_limit_bytes=16 * 2**20
         ),
         cost_estimate=pl.CostEstimate(flops=flops, bytes_accessed=size, transcendentals=0),
     )
@@ -100,10 +100,18 @@
     return jax.ShapeDtypeStruct(shape, BF)
 
 
-def pack(blk, pos, tile):
-    def body(blk_ref, pos_ref, left_in, upper_in, left_out, upper_out):
+def pack(blk, pos, tile, inverse):
+    def body(blk_ref, pos_ref, left_in, upper_in, quarter_in, left_out, upper_out, first, later):
         left_out[0] = left_in[0]
         upper_out[0] = upper_in[0]
+
+        @pl.when(pl.program_id(0) == 0)
+        def _():
+            first[0] = quarter_in[0, 0]
+
+        @pl.when(pl.program_id(0) > 0)
+        def _():
+            later[0] = quarter_in[0, 0]
 
     spec = pl.BlockSpec((1, 256, 256), lambda i, blk, pos: (i, 0, 0))
     return call(
@@ -118,79 +126,87 @@
                 (1, 256, 256),
                 lambda i, blk, pos: (0, row_pivot(blk, pos, 0), block_of(i, col_pivot(blk, pos, 0))),
             ),
+            pl.BlockSpec((1, 1, 256, 256), lambda i, blk, pos: (i, pos[1], 0, 0)),
         ],
-        [spec, spec],
-        [out((3, 256, 256)), out((3, 256, 256))],
+        [
+            spec,
+            spec,
+            whole((1, 256, 256)),
+            pl.BlockSpec((1, 256, 256), lambda i, blk, pos: (jnp.maximum(i - 1, 0), 0, 0)),
+        ],
+        [out((3, 256, 256)), out((3, 256, 256)), out((1, 256, 256)), out((2, 256, 256))],
         [],
-        size=2**20,
-    )(blk, pos, tile, tile)
+        size=2**21,
+    )(blk, pos, tile, tile, inverse)
 
 
 def join_inverse(blk, pos, levels, own, far, other, other_far):
     first, count = levels
 
     def body(blk_ref, pos_ref, dc, dz, oc, oz, d_ref):
-        c = pos_ref[2]
-        for flip, ref in zip((0, 2, 1, 3), (dc, dz, oc, oz)):
-            d_ref[0, :, pl.ds(pl.multiple_of((c ^ flip) * 256, 256), 256)] = ref[0, 0]
-
-    def far_map(flip):
-        return lambda n, k, blk, pos: (arrival(k, pos[1], pos[2] % 2 ^ flip), n, 0, 0)
-
-    near = pl.BlockSpec((1, 1, 256, 256), lambda n, k, blk, pos: (first + n, k, 0, 0))
-    return call(
-        body,
-        (count, 4),
-        [
-            near,
-            pl.BlockSpec((1, 1, 256, 256), far_map(0)),
-            near,
-            pl.BlockSpec((1, 1, 256, 256), far_map(1)),
-        ],
-        pl.BlockSpec((1, 256, 1024), lambda n, k, blk, pos: (n, k, 0)),
+        r, c = pos_ref[1], pos_ref[2]
+        for k in range(4):
+            rows = slice(k * 256, (k + 1) * 256)
+            for flip, piece in (
+                (0, dc[0, k]),
+                (2, dz[arrival(k, r, c % 2), 0]),
+                (1, oc[0, k]),
+                (3, oz[arrival(k, r, (c % 2) ^ 1), 0]),
+            ):
+                d_ref[0, rows, pl.ds(pl.multiple_of((c ^ flip) * 256, 256), 256)] = piece
+
+    near = pl.BlockSpec((1, 4, 256, 256), lambda n, blk, pos: (first + n, 0, 0, 0))
+    swapped = pl.BlockSpec((4, 1, 256, 256), lambda n, blk, pos: (0, n, 0, 0))
+    return call(
+        body,
+        (count,),
+        [near, swapped, near, swapped],
+        pl.BlockSpec((1, 1024, 1024), lambda n, blk, pos: (n, 0, 0)),
         out((count, 1024, 1024)),
         [],
         size=count * 2**22,
     )(blk, pos, own, far, other, other_far)
 
 
-def join_upper(blk, pos, pieces):
-    parts = len(pieces)
-    rows = 256 // parts
-
+def join_upper(blk, pos, pieces, halved=False):
     def body(blk_ref, pos_ref, *refs):
+        r, c = pos_ref[1], pos_ref[2]
         u_all = refs[-1]
-        r, c = pos_ref[1], pos_ref[2]
-        near_q = r ^ jnp.where(c % 2 == 0, 1, 3)
-        far_q = r ^ jnp.where(c % 2 == 0, 3, 1)
-        for h in range(parts):
-            u0, u1, u2 = refs[3 * h : 3 * h + 3]
+        lead = bit_of(pos_ref, 0) * 128
+        if len(refs) == 5:
+            parts = tuple(((r + n) & 3, ref) for n, ref in zip((0, 2, 3, 1), refs))
+        else:
+            near_q = r ^ jnp.where(c % 2 == 0, 1, 3)
+            far_q = r ^ jnp.where(c % 2 == 0, 3, 1)
+            parts = (r, refs[0]), (near_q, refs[1]), (far_q, refs[2].at[0]), (r ^ 2, refs[2].at[1])
+        for q, ref in parts:
             for s in range(3):
-                u_all[s, pl.ds(r * 256 + h * rows, rows)] = u0[s]
-                u_all[s, pl.ds(near_q * 256 + h * rows, rows)] = u1[s]
-                u_all[s, pl.ds(far_q * 256 + h * rows, rows)] = u2[0, s]
-                u_all[s, pl.ds((r ^ 2) * 256 + h * rows, rows)] = u2[1, s]
+                if halved:
+                    u_all[s, pl.ds(q * 256 + lead, 128)] = ref[s, :128]
+                    u_all[s, pl.ds(q * 256 + 128 - lead, 128)] = ref[s, 128:]
+                else:
+                    u_all[s, pl.ds(q * 256, 256)] = ref[s]
 
     return call(
         body,
         (1,),
-        [whole((3, rows, 256)), whole((3, rows, 256)), whole((2, 3, rows, 256))] * parts,
+        [whole(x.shape) for x in pieces],
         whole((3, 1024, 256)),
         out((3, 1024, 256)),
         [],
         size=3 * 2**20,
-    )(blk, pos, *[x for piece in pieces for x in piece])
+    )(blk, pos, *pieces)
 
 
 def scale(blk, pos, lane, lefts, inverse):
-    rows = lefts[0].shape[0]
-
-    def body(blk_ref, pos_ref, l0, l1, l2, l3, d_ref, s_ref, l_all):
+    rows = lefts[0].shape[1]
+
+    def body(blk_ref, pos_ref, own, other, d_ref, s_ref, l_all):
         c = pos_ref[2]
 
         @pl.when(pl.program_id(0) == 0)
         def _():
-            for flip, ref in zip((0, 2, 1, 3), (l0, l1, l2, l3)):
+            for flip, ref in zip((0, 2, 1, 3), (own.at[0], own.at[1], other.at[0], other.at[1])):
                 for i in range(rows):
                     l_all[i * 256 : (i + 1) * 256, pl.ds(pl.multiple_of((c ^ flip) * 256, 256), 256)] = ref[i]
 
@@ -199,7 +215,7 @@
     return call(
         body,
         (4,),
-        [whole((rows, 256, 256))] * 4
+        [whole((2, rows, 256, 256))] * 2
         + [pl.BlockSpec((1, 1024, 256), lambda q, blk, pos: (lane, 0, q))],
         pl.BlockSpec((rows * 256, 256), lambda q, blk, pos: (0, q)),
         out((rows * 256, 1024)),
@@ -232,7 +248,7 @@
         bit = bit_of(pos, 0)
         return jnp.where(i < 2, 2 * (1 - bit), 2 * bit) + (i & 1)
 
-    def body(blk_ref, pos_ref, x_ref, s_ref, u_ref, a0, a1, al, b0, b1, ks, kp, e_all):
+    def body(blk_ref, pos_ref, x_ref, s_ref, u_ref, au, al, b0, b1, ks, kp, e_all):
         i = pl.program_id(0)
         rb = row_block(i, pos_ref)
         for b in range(4):
@@ -261,12 +277,10 @@
         @pl.when(rb == row_pivot(blk_ref, pos_ref, 1))
         def _():
             for d in range(3):
-                a0[d] = e_all[block_of(d, nxt), :128]
-                a1[d] = e_all[block_of(d, nxt), 128:]
+                au[d] = e_all[block_of(d, nxt)]
 
     shapes = [
-        (3, 128, 256), (3, 128, 256), (2, 256, 256), (3, 256, 256), (3, 256, 256),
-        (2, 3, 256, 256), (2, 256, 256),
+        (3, 256, 256), (2, 256, 256), (3, 256, 256), (3, 256, 256), (2, 3, 256, 256), (2, 256, 256),
     ]
     return call(
         body,
@@ -290,13 +304,14 @@
 def update_second(blk, pos, ks, rb0, rb1, kp, ra, scaled, upper):
     def body(
         blk_ref, pos_ref, ks_ref, rb0_ref, rb1_ref, kp_ref, ra_ref, s_ref, u_ref,
-        a0, a1, al, bg, ks2, kp2, e_all,
+        given, kept, al, bg, ks2, kp2, e_all,
     ):
         pivot = col_pivot(blk_ref, pos_ref, 1)
         nxt = col_pivot(blk_ref, pos_ref, 2)
+        lead = bit_of(pos_ref, 0)
         for d in range(3):
-            a0[d] = jnp.zeros((128, 256), BF)
-            a1[d] = jnp.zeros((128, 256), BF)
+            given[d] = jnp.zeros((128, 256), BF)
+            kept[d] = jnp.zeros((128, 256), BF)
         for n, rb_ref in ((0, rb0_ref), (1, rb1_ref)):
             here = 2 * bit_of(pos_ref, 0) + n
             e_all[pivot] = (kp_ref[n].astype(F32) + ra_ref[n].astype(F32)).astype(BF)
@@ -320,8 +335,8 @@
             @pl.when(here == row_pivot(blk_ref, pos_ref, 2))
             def _():
                 for d in range(3):
-                    a0[d] = e_all[block_of(d, nxt), :128]
-                    a1[d] = e_all[block_of(d, nxt), 128:]
+                    given[d] = e_all[block_of(d, nxt), pl.ds((1 - lead) * 128, 128)]
+                    kept[d] = e_all[block_of(d, nxt), pl.ds(lead * 128, 128)]
 
     shapes = [
         (3, 128, 256), (3, 128, 256), (1, 256, 256), (3, 256, 256), (3, 256, 256), (1, 256, 256),
@@ -376,11 +391,19 @@
     return piece, near, far
 
 
+def ring_rows(piece):
+    rows = lax.axis_size("row")
+
+    def step(n):
+        route = lambda i: (i + n) % rows
+        return move(piece, ("row",), route)
+
+    return piece, step(2), step(1), step(3)
+
+
 def gather_left(piece):
-    far = far_half(piece)
-    own_other = other_core(piece)
-    far_other = other_core(far)
-    return piece, far, own_other, far_other
+    both = jnp.stack([piece, far_half(piece)])
+    return both, other_core(both)
 
 
 def far_inverse(part):
@@ -398,36 +421,34 @@
         [lax.axis_index("grid").astype(jnp.int32), row, lax.axis_index("col").astype(jnp.int32)]
     )
     inverse = d_inv.reshape(3, 4, 256, 256)
-    quarter = lax.dynamic_index_in_dim(inverse, row, 1, keepdims=False)
-
-    dz0, oz0 = far_inverse(quarter[:1])
-    left0, upper0 = pack(blk, pos, schur)
+    left0, upper0, first, later = pack(blk, pos, schur, inverse)
+    dz0, oz0 = far_inverse(first)
     d_other = other_core(inverse)
-    upper0 = join_upper(blk, pos, [spread_rows(upper0)])
+    upper0 = join_upper(blk, pos, spread_rows(upper0))
     lefts0 = gather_left(left0)
-    dz12, oz12 = far_inverse(quarter[1:])
+    dz12, oz12 = far_inverse(later)
     whole0 = join_inverse(blk, pos, (0, 1), inverse, dz0, d_other, oz0)
     whole12 = join_inverse(blk, pos, (1, 2), inverse, dz12, d_other, oz12)
 
     scaled0 = scale(blk, pos, 0, lefts0, whole0)
-    a0, a1, al, b0, b1, ks, kp = update_first(blk, pos, schur, scaled0, upper0)
-    u10 = total(a0, across(a0, 1))
+    au, al, b0, b1, ks, kp = update_first(blk, pos, schur, scaled0, upper0)
     ral = across(al, 1)
-    u11 = total(a1, across(a1, 1))
+    upper1 = total(au, across(au, 1))
     rb0 = across(b0, 1)
     rb1 = across(b1, 1)
-    upper1 = join_upper(blk, pos, [spread_rows(u10), spread_rows(u11)])
+    upper1 = join_upper(blk, pos, spread_rows(upper1))
     lefts1 = gather_left(total(kp, ral))
     scaled1 = scale(blk, pos, 0, lefts1, whole12)
-    a0, a1, al, bg, ks, kp = update_second(blk, pos, ks, rb0, rb1, kp, ral, scaled1, upper1)
-
-    u20 = total(a0, across(a0, 2))
-    u21 = total(a1, across(a1, 2))
+    given, kept, al, bg, ks, kp = update_second(
+        blk, pos, ks, rb0, rb1, kp, ral, scaled1, upper1
+    )
+
     ral = across(al, 2)
     rb = across(bg, 2)
-    u20 = total(u20, across(u20, 1))
-    u21 = total(u21, across(u21, 1))
-    upper2 = join_upper(blk, pos, [spread_rows(u20), spread_rows(u21)])
+    part = total(kept, across(given, 1))
+    part = total(part, across(part, 2))
+    upper2 = jnp.concatenate([part, across(part, 1)], axis=1)
+    upper2 = join_upper(blk, pos, ring_rows(upper2), True)
     lefts2 = gather_left(total(kp, ral))
     scaled2 = scale(blk, pos, 1, lefts2, whole12)
     give, keep = update_third(blk, pos, ks, rb, kp, ral, scaled2, upper2)

time: 238 us -> 220 us (0.924)
  the two profiles are of different devices: /device:TPU:1 before, /device:TPU:24 now
where the time goes in v2:
time: 220 us; the launch traced here: 219 us
  waiting for transfers between devices  98.1 us (45%)
  starting transfers between devices  94.9 us (43%)
  Pallas kernels  20.1 us (9%)
  local copies, waits for them, and re-layouts  3.69 us (2%)
    ppermute x32, waiting for transfers between devices, move(): return lax.ppermute(block, axes, [(i, route(i)) for i in range(count)])  98.1 us
    ppermute x32, starting transfers between devices, move(): return lax.ppermute(block, axes, [(i, route(i)) for i in range(count)])  94.9 us
    pallas_call x3, Pallas kernels, scale(): call(body, (4,), [whole((2, rows, 256, 256))] * 2 + [pl.BlockSpec((1, 102...  8.69 us
  transfers between devices with their start and end apart: 32, of which 16 were waited for; matrix products, arithmetic and copies ran while one was open for 1% of the time, Pallas kernels for 8%

profile of v2, /device:TPU:24, one launch (start us, length us, event | category | flops | bytes accessed | tf_op | source)
XLA Modules:
  0.0 219.1 jit_solution(6669800525092348418)
XLA Ops:
  6.7 3.4 %collective-permute-start.7 = (bf16[3,256,256]{2,1,0:T(8,128)(2,1)S(1)}, bf16[3,256,256]{2,1,0:T(8,128)(2,1)S(1)}, u32[]{:S(2)}, u32[]{:S(2)}) collective-permute-start(bf16[3,256,256]{2,1,0:T(8,128)(2,1)S(1)} %get-tuple-element.25.refs_0_), channel_id=1, source_target_pairs={{0,4},{1,13},{2,6},{3,15},{4,0},{5,9},{6,2},{7,11},{8,12},{9,5},{1... | collective-permute-start | bytes 1179656 | tf_op jit(solution)/shard_map/ppermute | solution.py:18
  10.1 10.9 %collective-permute-start.2 = (bf16[1,256,256]{2,1,0:T(8,128)(2,1)S(1)}, bf16[1,256,256]{2,1,0:T(8,128)(2,1)S(1)}, u32[]{:S(2)}, u32[]{:S(2)}) collective-permute-start(bf16[1,256,256]{2,1,0:T(8,128)(2,1)S(1)} %get-tuple-element.24), channel_id=1, source_target_pairs={{0,2},{1,3},{2,0},{3,1},{4,6},{5,7},{6,4},{7,5},{8,10},{9,11},{10,... | collective-permute-start | bytes 393224 | tf_op jit(solution)/shard_map/ppermute | solution.py:18
  24.7 2.7 %collective-permute-start.3 = (bf16[1,256,256]{2,1,0:T(8,128)(2,1)S(1)}, bf16[1,256,256]{2,1,0:T(8,128)(2,1)S(1)}, u32[]{:S(2)}, u32[]{:S(2)}) collective-permute-start(bf16[1,256,256]{2,1,0:T(8,128)(2,1)S(1)} %collective-permute-done.2), channel_id=1, source_target_pairs={{0,4},{1,13},{2,6},{3,15},{4,0},{5,9},{6,2},{7,11},{8,12},{9,5},{1... | collective-permute-start | bytes 393224 | tf_op jit(solution)/shard_map/ppermute | solution.py:18
  27.4 4.1 %collective-permute-done.3 = bf16[1,256,256]{2,1,0:T(8,128)(2,1)S(1)} collective-permute-done((bf16[1,256,256]{2,1,0:T(8,128)(2,1)S(1)}, bf16[1,256,256]{2,1,0:T(8,128)(2,1)S(1)}, u32[]{:S(2)}, u32[]{:S(2)}) %collective-permute-start.3) | collective-permute-done | bytes 131104 | tf_op jit(solution)/shard_map/ppermute | solution.py:18
  31.5 6.9 %collective-permute-start.4 = (bf16[2,1,256,256]{3,2,1,0:T(8,128)(2,1)S(1)}, bf16[2,1,256,256]{3,2,1,0:T(8,128)(2,1)S(1)}, u32[]{:S(2)}, u32[]{:S(2)}) collective-permute-start(bf16[2,1,256,256]{3,2,1,0:T(8,128)(2,1)S(1)} %pad_maximum_fusion.8), channel_id=1, source_target_pairs={{0,12},{1,5},{2,14},{3,7},{4,8},{5,1},{6,10},{7,3},{8,4},{9,13},{1... | collective-permute-start | bytes 786440 | tf_op jit(solution)/shard_map/ppermute | solution.py:18
  40.4 9.5 %collective-permute-done = bf16[3,256,256]{2,1,0:T(8,128)(2,1)S(1)} collective-permute-done((bf16[3,256,256]{2,1,0:T(8,128)(2,1)S(1)}, bf16[3,256,256]{2,1,0:T(8,128)(2,1)S(1)}, u32[]{:S(2)}, u32[]{:S(2)}) %collective-permute-start) | collective-permute-done | bytes 393248 | tf_op jit(solution)/shard_map/ppermute | solution.py:18
  54.4 2.8 %collective-permute-start.14 = (bf16[2,256,256]{2,1,0:T(8,128)(2,1)S(1)}, bf16[2,256,256]{2,1,0:T(8,128)(2,1)S(1)}, u32[]{:S(2)}, u32[]{:S(2)}) collective-permute-start(bf16[2,256,256]{2,1,0:T(8,128)(2,1)S(1)} %get-tuple-element.31), channel_id=1, source_target_pairs={{0,2},{1,3},{2,0},{3,1},{4,6},{5,7},{6,4},{7,5},{8,10},{9,11},{10,... | collective-permute-start | bytes 786440 | tf_op jit(solution)/shard_map/ppermute | solution.py:18
  57.2 15.7 %collective-permute-done.14 = bf16[2,256,256]{2,1,0:T(8,128)(2,1)S(1)} collective-permute-done((bf16[2,256,256]{2,1,0:T(8,128)(2,1)S(1)}, bf16[2,256,256]{2,1,0:T(8,128)(2,1)S(1)}, u32[]{:S(2)}, u32[]{:S(2)}) %collective-permute-start.14) | collective-permute-done | bytes 262176 | tf_op jit(solution)/shard_map/ppermute | solution.py:18
  72.9 2.6 %collective-permute-start.15 = (bf16[2,256,256]{2,1,0:T(8,128)(2,1)S(1)}, bf16[2,256,256]{2,1,0:T(8,128)(2,1)S(1)}, u32[]{:S(2)}, u32[]{:S(2)}) collective-permute-start(bf16[2,256,256]{2,1,0:T(8,128)(2,1)S(1)} %collective-permute-done.14), channel_id=1, source_target_pairs={{0,4},{1,13},{2,6},{3,15},{4,0},{5,9},{6,2},{7,11},{8,12},{9,5},{1... | collective-permute-start | bytes 786440 | tf_op jit(solution)/shard_map/ppermute | solution.py:18
  77.1 3.5 %shard_map.39.s_ref = bf16[768,1024]{1,0:T(8,128)(2,1)S(1)} custom-call(s32[3,12]{1,0:T(4,128)S(1)} %bitcast.35, s32[3]{0:T(128)S(1)} %pad_add_fusion.pos_ref, bf16[2,3,256,256]{3,2,1,0:T(8,128)(2,1)S(1)} %pad_maximum_fusion.1.own, bf16[2,3,256,256]{3,2,1,0:T(8,128)(2,1)S(1)} %collective-permute-done.1.other, bf16[1,1024,1024]{2,1,0:T(8,128)(2,1)S(1)} %shard_map.38.d_ref), custom_call_target="tpu_custom_call" | custom-call | flops 1610612736 | bytes 4194304 | tf_op jit(solution)/shard_map/pallas_call | solution.py:215
  80.7 3.9 %shard_map.41 = (bf16[3,256,256]{2,1,0:T(8,128)(2,1)S(1)}, bf16[2,256,256]{2,1,0:T(8,128)(2,1)S(1)}, bf16[3,256,256]{2,1,0:T(8,128)(2,1)S(1)}, bf16[3,256,256]{2...) custom-call(s32[3,12]{1,0:T(4,128)S(1)} %bitcast.36, ...), custom_call_target="tpu_custom_call" | custom-call | flops 1207959552 | bytes 8388608 | tf_op jit(solution)/shard_map/pallas_call | solution.py:285
  86.5 2.5 %collective-permute-start.16 = (bf16[2,2,256,256]{3,2,1,0:T(8,128)(2,1)S(1)}, bf16[2,2,256,256]{3,2,1,0:T(8,128)(2,1)S(1)}, u32[]{:S(2)}, u32[]{:S(2)}) collective-permute-start(bf16[2,2,256,256]{3,2,1,0:T(8,128)(2,1)S(1)} %pad_maximum_fusion.6), channel_id=1, source_target_pairs={{0,12},{1,5},{2,14},{3,7},{4,8},{5,1},{6,10},{7,3},{8,4},{9,13},{1... | collective-permute-start | bytes 1572872 | tf_op jit(solution)/shard_map/ppermute | solution.py:18
  89.1 3.9 %collective-permute-start.11 = (bf16[2,256,256]{2,1,0:T(8,128)(2,1)S(1)}, bf16[2,256,256]{2,1,0:T(8,128)(2,1)S(1)}, u32[]{:S(2)}, u32[]{:S(2)}) collective-permute-start(bf16[2,256,256]{2,1,0:T(8,128)(2,1)S(1)} %get-tuple-element.30), channel_id=1, source_target_pairs={{0,16},{16,0},{32,48},{48,32},{64,80},{80,64},{96,112},{112,96},{1... | collective-permute-start | bytes 786440 | tf_op jit(solution)/shard_map/ppermute | solution.py:18
  93.0 5.4 %collective-permute-done.18 = bf16[3,256,256]{2,1,0:T(8,128)(2,1)S(1)} collective-permute-done((bf16[3,256,256]{2,1,0:T(8,128)(2,1)S(1)}, bf16[3,256,256]{2,1,0:T(8,128)(2,1)S(1)}, u32[]{:S(2)}, u32[]{:S(2)}) %collective-permute-start.18) | collective-permute-done | bytes 393248 | tf_op jit(solution)/shard_map/ppermute | solution.py:18
  104.9 3.3 %collective-permute-done.19.refs_1_ = bf16[3,256,256]{2,1,0:T(8,128)(2,1)S(1)} collective-permute-done((bf16[3,256,256]{2,1,0:T(8,128)(2,1)S(1)}, bf16[3,256,256]{2,1,0:T(8,128)(2,1)S(1)}, u32[]{:S(2)}, u32[]{:S(2)}) %collective-permute-start.19) | collective-permute-done | bytes 393248 | tf_op jit(solution)/shard_map/ppermute | solution.py:18
  110.8 11.5 %collective-permute-done.12 = bf16[2,256,256]{2,1,0:T(8,128)(2,1)S(1)} collective-permute-done((bf16[2,256,256]{2,1,0:T(8,128)(2,1)S(1)}, bf16[2,256,256]{2,1,0:T(8,128)(2,1)S(1)}, u32[]{:S(2)}, u32[]{:S(2)}) %collective-permute-start.12) | collective-permute-done | bytes 262176 | tf_op jit(solution)/shard_map/ppermute | solution.py:18
  124.3 2.7 %collective-permute-start.9 = (bf16[3,256,256]{2,1,0:T(8,128)(2,1)S(1)}, bf16[3,256,256]{2,1,0:T(8,128)(2,1)S(1)}, u32[]{:S(2)}, u32[]{:S(2)}) collective-permute-start(bf16[3,256,256]{2,1,0:T(8,128)(2,1)S(1)} %get-tuple-element.27), channel_id=1, source_target_pairs={{0,16},{16,0},{32,48},{48,32},{64,80},{80,64},{96,112},{112,96},{1... | collective-permute-start | bytes 1179656 | tf_op jit(solution)/shard_map/ppermute | solution.py:18
  127.0 3.1 %collective-permute-start.10 = (bf16[3,256,256]{2,1,0:T(8,128)(2,1)S(1)}, bf16[3,256,256]{2,1,0:T(8,128)(2,1)S(1)}, u32[]{:S(2)}, u32[]{:S(2)}) collective-permute-start(bf16[3,256,256]{2,1,0:T(8,128)(2,1)S(1)} %get-tuple-element.28), channel_id=1, source_target_pairs={{0,16},{16,0},{32,48},{48,32},{64,80},{80,64},{96,112},{112,96},{1... | collective-permute-start | bytes 1179656 | tf_op jit(solution)/shard_map/ppermute | solution.py:18
  131.5 2.9 %shard_map.43.s_ref = bf16[512,1024]{1,0:T(8,128)(2,1)S(1)} custom-call(s32[3,12]{1,0:T(4,128)S(1)} %bitcast.38, s32[3]{0:T(128)S(1)} %pad_add_fusion.pos_ref, bf16[2,2,256,256]{3,2,1,0:T(8,128)(2,1)S(1)} %pad_maximum_fusion.5.own, bf16[2,2,256,256]{3,2,1,0:T(8,128)(2,1)S(1)} %collective-permute-done.13.other, bf16[2,1024,1024]{2,1,0:T(8,128)(2,1)S(1)} %shard_map.42.d_ref), custom_call_target="tpu_custom_call" | custom-call | flops 1073741824 | bytes 4194304 | tf_op jit(solution)/shard_map/pallas_call | solution.py:215
  135.0 3.1 %collective-permute-done.9.rb0_ref = bf16[3,256,256]{2,1,0:T(8,128)(2,1)S(1)} collective-permute-done((bf16[3,256,256]{2,1,0:T(8,128)(2,1)S(1)}, bf16[3,256,256]{2,1,0:T(8,128)(2,1)S(1)}, u32[]{:S(2)}, u32[]{:S(2)}) %collective-permute-start.9) | collective-permute-done | bytes 393248 | tf_op jit(solution)/shard_map/ppermute | solution.py:18
  138.1 8.0 %collective-permute-done.10.rb1_ref = bf16[3,256,256]{2,1,0:T(8,128)(2,1)S(1)} collective-permute-done((bf16[3,256,256]{2,1,0:T(8,128)(2,1)S(1)}, bf16[3,256,256]{2,1,0:T(8,128)(2,1)S(1)}, u32[]{:S(2)}, u32[]{:S(2)}) %collective-permute-start.10) | collective-permute-done | bytes 393248 | tf_op jit(solution)/shard_map/ppermute | solution.py:18
  147.7 2.7 %collective-permute-start.25 = (bf16[3,128,256]{2,1,0:T(8,128)(2,1)S(1)}, bf16[3,128,256]{2,1,0:T(8,128)(2,1)S(1)}, u32[]{:S(2)}, u32[]{:S(2)}) collective-permute-start(bf16[3,128,256]{2,1,0:T(8,128)(2,1)S(1)} %get-tuple-element.38), channel_id=1, source_target_pairs={{0,16},{16,0},{32,48},{48,32},{64,80},{80,64},{96,112},{112,96},{1... | collective-permute-start | bytes 589832 | tf_op jit(solution)/shard_map/ppermute | solution.py:18
  150.4 5.9 %collective-permute-done.25 = bf16[3,128,256]{2,1,0:T(8,128)(2,1)S(1)} collective-permute-done((bf16[3,128,256]{2,1,0:T(8,128)(2,1)S(1)}, bf16[3,128,256]{2,1,0:T(8,128)(2,1)S(1)}, u32[]{:S(2)}, u32[]{:S(2)}) %collective-permute-start.25) | collective-permute-done | bytes 196640 | tf_op jit(solution)/shard_map/ppermute | solution.py:18
  158.3 4.8 %collective-permute-start.22 = (bf16[1,256,256]{2,1,0:T(8,128)(2,1)S(1)}, bf16[1,256,256]{2,1,0:T(8,128)(2,1)S(1)}, u32[]{:S(2)}, u32[]{:S(2)}) collective-permute-start(bf16[1,256,256]{2,1,0:T(8,128)(2,1)S(1)} %get-tuple-element.36), channel_id=1, source_target_pairs={{0,32},{16,48},{32,0},{48,16},{64,96},{80,112},{96,64},{112,80},{1... | collective-permute-start | bytes 393224 | tf_op jit(solution)/shard_map/ppermute | solution.py:18
  163.1 9.2 %collective-permute-done.26 = bf16[3,128,256]{2,1,0:T(8,128)(2,1)S(1)} collective-permute-done((bf16[3,128,256]{2,1,0:T(8,128)(2,1)S(1)}, bf16[3,128,256]{2,1,0:T(8,128)(2,1)S(1)}, u32[]{:S(2)}, u32[]{:S(2)}) %collective-permute-start.26) | collective-permute-done | bytes 196640 | tf_op jit(solution)/shard_map/ppermute | solution.py:18
  177.4 3.2 %collective-permute-start.21 = (bf16[3,256,256]{2,1,0:T(8,128)(2,1)S(1)}, bf16[3,256,256]{2,1,0:T(8,128)(2,1)S(1)}, u32[]{:S(2)}, u32[]{:S(2)}) collective-permute-start(bf16[3,256,256]{2,1,0:T(8,128)(2,1)S(1)} %get-tuple-element.34), channel_id=1, source_target_pairs={{0,32},{16,48},{32,0},{48,16},{64,96},{80,112},{96,64},{112,80},{1... | collective-permute-start | bytes 1179656 | tf_op jit(solution)/shard_map/ppermute | solution.py:18
  180.6 4.7 %collective-permute-done.27 = bf16[3,128,256]{2,1,0:T(8,128)(2,1)S(1)} collective-permute-done((bf16[3,128,256]{2,1,0:T(8,128)(2,1)S(1)}, bf16[3,128,256]{2,1,0:T(8,128)(2,1)S(1)}, u32[]{:S(2)}, u32[]{:S(2)}) %collective-permute-start.27) | collective-permute-done | bytes 196640 | tf_op jit(solution)/shard_map/ppermute | solution.py:18
  185.3 2.6 %collective-permute-start.30 = (bf16[3,256,256]{2,1,0:T(8,128)(2,1)S(1)}, bf16[3,256,256]{2,1,0:T(8,128)(2,1)S(1)}, u32[]{:S(2)}, u32[]{:S(2)}) collective-permute-start(bf16[3,256,256]{2,1,0:T(8,128)(2,1)S(1)} %pad_maximum_fusion.7.refs_0_), channel_id=1, source_target_pairs={{0,12},{4,0},{8,4},{12,8},{1,13},{5,1},{9,5},{13,9},{2,14},{6,2},{... | collective-permute-start | bytes 1179656 | tf_op jit(solution)/shard_map/ppermute | solution.py:18
  187.9 3.3 %collective-permute-start.29 = (bf16[3,256,256]{2,1,0:T(8,128)(2,1)S(1)}, bf16[3,256,256]{2,1,0:T(8,128)(2,1)S(1)}, u32[]{:S(2)}, u32[]{:S(2)}) collective-permute-start(bf16[3,256,256]{2,1,0:T(8,128)(2,1)S(1)} %pad_maximum_fusion.7.refs_0_), channel_id=1, source_target_pairs={{0,4},{4,8},{8,12},{12,0},{1,5},{5,9},{9,13},{13,1},{2,6},{6,10},{... | collective-permute-start | bytes 1179656 | tf_op jit(solution)/shard_map/ppermute | solution.py:18
  191.2 4.0 %collective-permute-start.28 = (bf16[3,256,256]{2,1,0:T(8,128)(2,1)S(1)}, bf16[3,256,256]{2,1,0:T(8,128)(2,1)S(1)}, u32[]{:S(2)}, u32[]{:S(2)}) collective-permute-start(bf16[3,256,256]{2,1,0:T(8,128)(2,1)S(1)} %pad_maximum_fusion.7.refs_0_), channel_id=1, source_target_pairs={{0,8},{4,12},{8,0},{12,4},{1,9},{5,13},{9,1},{13,5},{2,10},{6,14},... | collective-permute-start | bytes 1179656 | tf_op jit(solution)/shard_map/ppermute | solution.py:18
  201.0 7.6 %collective-permute-done.28.refs_1_ = bf16[3,256,256]{2,1,0:T(8,128)(2,1)S(1)} collective-permute-done((bf16[3,256,256]{2,1,0:T(8,128)(2,1)S(1)}, bf16[3,256,256]{2,1,0:T(8,128)(2,1)S(1)}, u32[]{:S(2)}, u32[]{:S(2)}) %collective-permute-start.28) | collective-permute-done | bytes 393248 | tf_op jit(solution)/shard_map/ppermute | solution.py:18
  212.0 6.3 %collective-permute-done.31 = bf16[128,1024]{1,0:T(8,128)(2,1)S(1)} collective-permute-done((bf16[128,1024]{1,0:T(8,128)(2,1)S(1)}, bf16[128,1024]{1,0:T(8,128)(2,1)S(1)}, u32[]{:S(2)}, u32[]{:S(2)}) %collective-permute-start.31) | collective-permute-done | bytes 262176 | tf_op jit(solution)/shard_map/ppermute | solution.py:18
  (70 shorter events, 51.8 us)
Async XLA Ops:
  0.0 76.2 %collective-permute-start.5 = (bf16[3,4,256,256]{3,2,1,0:T(8,128)(2,1)}, bf16[3,4,256,256]{3,2,1,0:T(8,128)(2,1)S(1)}, u32[]{:S(2)}, u32[]{:S(2)}) collective-permute-start(bf16[3,4,256,256]{3,2,1,0:T(8,128)(2,1)} %bitcast.23), channel_id=1, source_target_pairs={{0,1},{1,0},{2,3},{3,2},{4,5},{5,4},{6,7},{7,6},{8,9},{9,8},{10,11... | collective-permute-start | bytes 4718600 | tf_op jit(solution)/shard_map/ppermute | solution.py:18
  6.7 31.7 %collective-permute-start.7 = (bf16[3,256,256]{2,1,0:T(8,128)(2,1)S(1)}, bf16[3,256,256]{2,1,0:T(8,128)(2,1)S(1)}, u32[]{:S(2)}, u32[]{:S(2)}) collective-permute-start(bf16[3,256,256]{2,1,0:T(8,128)(2,1)S(1)} %get-tuple-element.25.refs_0_), channel_id=1, source_target_pairs={{0,4},{1,13},{2,6},{3,15},{4,0},{5,9},{6,2},{7,11},{8,12},{9,5},{1... | collective-permute-start | bytes 1179656 | tf_op jit(solution)/shard_map/ppermute | solution.py:18
  10.1 14.6 %collective-permute-start.2 = (bf16[1,256,256]{2,1,0:T(8,128)(2,1)S(1)}, bf16[1,256,256]{2,1,0:T(8,128)(2,1)S(1)}, u32[]{:S(2)}, u32[]{:S(2)}) collective-permute-start(bf16[1,256,256]{2,1,0:T(8,128)(2,1)S(1)} %get-tuple-element.24), channel_id=1, source_target_pairs={{0,2},{1,3},{2,0},{3,1},{4,6},{5,7},{6,4},{7,5},{8,10},{9,11},{10,... | collective-permute-start | bytes 393224 | tf_op jit(solution)/shard_map/ppermute | solution.py:18
  21.0 28.9 %collective-permute-start = (bf16[3,256,256]{2,1,0:T(8,128)(2,1)S(1)}, bf16[3,256,256]{2,1,0:T(8,128)(2,1)S(1)}, u32[]{:S(2)}, u32[]{:S(2)}) collective-permute-start(bf16[3,256,256]{2,1,0:T(8,128)(2,1)S(1)} %get-tuple-element.23), channel_id=1, source_target_pairs={{0,2},{1,3},{2,0},{3,1},{4,6},{5,7},{6,4},{7,5},{8,10},{9,11},{10,... | collective-permute-start | bytes 1179656 | tf_op jit(solution)/shard_map/ppermute | solution.py:18
  24.7 6.8 %collective-permute-start.3 = (bf16[1,256,256]{2,1,0:T(8,128)(2,1)S(1)}, bf16[1,256,256]{2,1,0:T(8,128)(2,1)S(1)}, u32[]{:S(2)}, u32[]{:S(2)}) collective-permute-start(bf16[1,256,256]{2,1,0:T(8,128)(2,1)S(1)} %collective-permute-done.2), channel_id=1, source_target_pairs={{0,4},{1,13},{2,6},{3,15},{4,0},{5,9},{6,2},{7,11},{8,12},{9,5},{1... | collective-permute-start | bytes 393224 | tf_op jit(solution)/shard_map/ppermute | solution.py:18
  31.5 20.4 %collective-permute-start.4 = (bf16[2,1,256,256]{3,2,1,0:T(8,128)(2,1)S(1)}, bf16[2,1,256,256]{3,2,1,0:T(8,128)(2,1)S(1)}, u32[]{:S(2)}, u32[]{:S(2)}) collective-permute-start(bf16[2,1,256,256]{3,2,1,0:T(8,128)(2,1)S(1)} %pad_maximum_fusion.8), channel_id=1, source_target_pairs={{0,12},{1,5},{2,14},{3,7},{4,8},{5,1},{6,10},{7,3},{8,4},{9,13},{1... | collective-permute-start | bytes 786440 | tf_op jit(solution)/shard_map/ppermute | solution.py:18
  38.5 37.0 %collective-permute-start.8 = (bf16[2,3,256,256]{3,2,1,0:T(8,128)(2,1)S(1)}, bf16[2,3,256,256]{3,2,1,0:T(8,128)(2,1)S(1)}, u32[]{:S(2)}, u32[]{:S(2)}) collective-permute-start(bf16[2,3,256,256]{3,2,1,0:T(8,128)(2,1)S(1)} %pad_maximum_fusion.2), channel_id=1, source_target_pairs={{0,12},{1,5},{2,14},{3,7},{4,8},{5,1},{6,10},{7,3},{8,4},{9,13},{1... | collective-permute-start | bytes 2359304 | tf_op jit(solution)/shard_map/ppermute | solution.py:18
  50.0 27.1 %collective-permute-start.1 = (bf16[2,3,256,256]{3,2,1,0:T(8,128)(2,1)S(1)}, bf16[2,3,256,256]{3,2,1,0:T(8,128)(2,1)S(1)}, u32[]{:S(2)}, u32[]{:S(2)}) collective-permute-start(bf16[2,3,256,256]{3,2,1,0:T(8,128)(2,1)S(1)} %pad_maximum_fusion.1.own), channel_id=1, source_target_pairs={{0,1},{1,0},{2,3},{3,2},{4,5},{5,4},{6,7},{7,6},{8,9},{9,8},{10,11... | collective-permute-start | bytes 2359304 | tf_op jit(solution)/shard_map/ppermute | solution.py:18
  52.0 24.2 %collective-permute-start.6 = (bf16[4,1,256,256]{3,2,1,0:T(8,128)(2,1)S(1)}, bf16[4,1,256,256]{3,2,1,0:T(8,128)(2,1)S(1)}, u32[]{:S(2)}, u32[]{:S(2)}) collective-permute-start(bf16[4,1,256,256]{3,2,1,0:T(8,128)(2,1)S(1)} %pad_maximum_fusion.4.dz), channel_id=1, source_target_pairs={{0,1},{1,0},{2,3},{3,2},{4,5},{5,4},{6,7},{7,6},{8,9},{9,8},{10,11... | collective-permute-start | bytes 1572872 | tf_op jit(solution)/shard_map/ppermute | solution.py:18
  54.4 18.5 %collective-permute-start.14 = (bf16[2,256,256]{2,1,0:T(8,128)(2,1)S(1)}, bf16[2,256,256]{2,1,0:T(8,128)(2,1)S(1)}, u32[]{:S(2)}, u32[]{:S(2)}) collective-permute-start(bf16[2,256,256]{2,1,0:T(8,128)(2,1)S(1)} %get-tuple-element.31), channel_id=1, source_target_pairs={{0,2},{1,3},{2,0},{3,1},{4,6},{5,7},{6,4},{7,5},{8,10},{9,11},{10,... | collective-permute-start | bytes 786440 | tf_op jit(solution)/shard_map/ppermute | solution.py:18
  72.9 13.5 %collective-permute-start.15 = (bf16[2,256,256]{2,1,0:T(8,128)(2,1)S(1)}, bf16[2,256,256]{2,1,0:T(8,128)(2,1)S(1)}, u32[]{:S(2)}, u32[]{:S(2)}) collective-permute-start(bf16[2,256,256]{2,1,0:T(8,128)(2,1)S(1)} %collective-permute-done.14), channel_id=1, source_target_pairs={{0,4},{1,13},{2,6},{3,15},{4,0},{5,9},{6,2},{7,11},{8,12},{9,5},{1... | collective-permute-start | bytes 786440 | tf_op jit(solution)/shard_map/ppermute | solution.py:18
  84.5 13.9 %collective-permute-start.18 = (bf16[3,256,256]{2,1,0:T(8,128)(2,1)S(1)}, bf16[3,256,256]{2,1,0:T(8,128)(2,1)S(1)}, u32[]{:S(2)}, u32[]{:S(2)}) collective-permute-start(bf16[3,256,256]{2,1,0:T(8,128)(2,1)S(1)} %get-tuple-element.32), channel_id=1, source_target_pairs={{0,16},{16,0},{32,48},{48,32},{64,80},{80,64},{96,112},{112,96},{1... | collective-permute-start | bytes 1179656 | tf_op jit(solution)/shard_map/ppermute | solution.py:18
  86.5 14.2 %collective-permute-start.16 = (bf16[2,2,256,256]{3,2,1,0:T(8,128)(2,1)S(1)}, bf16[2,2,256,256]{3,2,1,0:T(8,128)(2,1)S(1)}, u32[]{:S(2)}, u32[]{:S(2)}) collective-permute-start(bf16[2,2,256,256]{3,2,1,0:T(8,128)(2,1)S(1)} %pad_maximum_fusion.6), channel_id=1, source_target_pairs={{0,12},{1,5},{2,14},{3,7},{4,8},{5,1},{6,10},{7,3},{8,4},{9,13},{1... | collective-permute-start | bytes 1572872 | tf_op jit(solution)/shard_map/ppermute | solution.py:18
  89.1 13.8 %collective-permute-start.11 = (bf16[2,256,256]{2,1,0:T(8,128)(2,1)S(1)}, bf16[2,256,256]{2,1,0:T(8,128)(2,1)S(1)}, u32[]{:S(2)}, u32[]{:S(2)}) collective-permute-start(bf16[2,256,256]{2,1,0:T(8,128)(2,1)S(1)} %get-tuple-element.30), channel_id=1, source_target_pairs={{0,16},{16,0},{32,48},{48,32},{64,80},{80,64},{96,112},{112,96},{1... | collective-permute-start | bytes 786440 | tf_op jit(solution)/shard_map/ppermute | solution.py:18
  98.5 9.7 %collective-permute-start.19 = (bf16[3,256,256]{2,1,0:T(8,128)(2,1)S(1)}, bf16[3,256,256]{2,1,0:T(8,128)(2,1)S(1)}, u32[]{:S(2)}, u32[]{:S(2)}) collective-permute-start(bf16[3,256,256]{2,1,0:T(8,128)(2,1)S(1)} %add_convert_fusion.refs_0_), channel_id=1, source_target_pairs={{0,4},{1,13},{2,6},{3,15},{4,0},{5,9},{6,2},{7,11},{8,12},{9,5},{1... | collective-permute-start | bytes 1179656 | tf_op jit(solution)/shard_map/ppermute | solution.py:18
  100.9 29.2 %collective-permute-start.17 = (bf16[4,2,256,256]{3,2,1,0:T(8,128)(2,1)S(1)}, bf16[4,2,256,256]{3,2,1,0:T(8,128)(2,1)S(1)}, u32[]{:S(2)}, u32[]{:S(2)}) collective-permute-start(bf16[4,2,256,256]{3,2,1,0:T(8,128)(2,1)S(1)} %pad_maximum_fusion.dz), channel_id=1, source_target_pairs={{0,1},{1,0},{2,3},{3,2},{4,5},{5,4},{6,7},{7,6},{8,9},{9,8},{10,11... | collective-permute-start | bytes 3145736 | tf_op jit(solution)/shard_map/ppermute | solution.py:18
  102.9 19.3 %collective-permute-start.12 = (bf16[2,256,256]{2,1,0:T(8,128)(2,1)S(1)}, bf16[2,256,256]{2,1,0:T(8,128)(2,1)S(1)}, u32[]{:S(2)}, u32[]{:S(2)}) collective-permute-start(bf16[2,256,256]{2,1,0:T(8,128)(2,1)S(1)} %add_convert_fusion.2), channel_id=1, source_target_pairs={{0,2},{1,3},{2,0},{3,1},{4,6},{5,7},{6,4},{7,5},{8,10},{9,11},{10,... | collective-permute-start | bytes 786440 | tf_op jit(solution)/shard_map/ppermute | solution.py:18
  108.3 26.1 %collective-permute-start.20 = (bf16[2,3,256,256]{3,2,1,0:T(8,128)(2,1)S(1)}, bf16[2,3,256,256]{3,2,1,0:T(8,128)(2,1)S(1)}, u32[]{:S(2)}, u32[]{:S(2)}) collective-permute-start(bf16[2,3,256,256]{3,2,1,0:T(8,128)(2,1)S(1)} %pad_maximum_fusion.3), channel_id=1, source_target_pairs={{0,12},{1,5},{2,14},{3,7},{4,8},{5,1},{6,10},{7,3},{8,4},{9,13},{1... | collective-permute-start | bytes 2359304 | tf_op jit(solution)/shard_map/ppermute | solution.py:18
  122.3 9.1 %collective-permute-start.13 = (bf16[2,2,256,256]{3,2,1,0:T(8,128)(2,1)S(1)}, bf16[2,2,256,256]{3,2,1,0:T(8,128)(2,1)S(1)}, u32[]{:S(2)}, u32[]{:S(2)}) collective-permute-start(bf16[2,2,256,256]{3,2,1,0:T(8,128)(2,1)S(1)} %pad_maximum_fusion.5.own), channel_id=1, source_target_pairs={{0,1},{1,0},{2,3},{3,2},{4,5},{5,4},{6,7},{7,6},{8,9},{9,8},{10,11... | collective-permute-start | bytes 1572872 | tf_op jit(solution)/shard_map/ppermute | solution.py:18
  124.3 13.9 %collective-permute-start.9 = (bf16[3,256,256]{2,1,0:T(8,128)(2,1)S(1)}, bf16[3,256,256]{2,1,0:T(8,128)(2,1)S(1)}, u32[]{:S(2)}, u32[]{:S(2)}) collective-permute-start(bf16[3,256,256]{2,1,0:T(8,128)(2,1)S(1)} %get-tuple-element.27), channel_id=1, source_target_pairs={{0,16},{16,0},{32,48},{48,32},{64,80},{80,64},{96,112},{112,96},{1... | collective-permute-start | bytes 1179656 | tf_op jit(solution)/shard_map/ppermute | solution.py:18
  127.0 19.1 %collective-permute-start.10 = (bf16[3,256,256]{2,1,0:T(8,128)(2,1)S(1)}, bf16[3,256,256]{2,1,0:T(8,128)(2,1)S(1)}, u32[]{:S(2)}, u32[]{:S(2)}) collective-permute-start(bf16[3,256,256]{2,1,0:T(8,128)(2,1)S(1)} %get-tuple-element.28), channel_id=1, source_target_pairs={{0,16},{16,0},{32,48},{48,32},{64,80},{80,64},{96,112},{112,96},{1... | collective-permute-start | bytes 1179656 | tf_op jit(solution)/shard_map/ppermute | solution.py:18
  147.7 8.6 %collective-permute-start.25 = (bf16[3,128,256]{2,1,0:T(8,128)(2,1)S(1)}, bf16[3,128,256]{2,1,0:T(8,128)(2,1)S(1)}, u32[]{:S(2)}, u32[]{:S(2)}) collective-permute-start(bf16[3,128,256]{2,1,0:T(8,128)(2,1)S(1)} %get-tuple-element.38), channel_id=1, source_target_pairs={{0,16},{16,0},{32,48},{48,32},{64,80},{80,64},{96,112},{112,96},{1... | collective-permute-start | bytes 589832 | tf_op jit(solution)/shard_map/ppermute | solution.py:18
  156.4 16.0 %collective-permute-start.26 = (bf16[3,128,256]{2,1,0:T(8,128)(2,1)S(1)}, bf16[3,128,256]{2,1,0:T(8,128)(2,1)S(1)}, u32[]{:S(2)}, u32[]{:S(2)}) collective-permute-start(bf16[3,128,256]{2,1,0:T(8,128)(2,1)S(1)} %add_convert_fusion.4), channel_id=1, source_target_pairs={{0,32},{16,48},{32,0},{48,16},{64,96},{80,112},{96,64},{112,80},{1... | collective-permute-start | bytes 589832 | tf_op jit(solution)/shard_map/ppermute | solution.py:18
  158.3 16.6 %collective-permute-start.22 = (bf16[1,256,256]{2,1,0:T(8,128)(2,1)S(1)}, bf16[1,256,256]{2,1,0:T(8,128)(2,1)S(1)}, u32[]{:S(2)}, u32[]{:S(2)}) collective-permute-start(bf16[1,256,256]{2,1,0:T(8,128)(2,1)S(1)} %get-tuple-element.36), channel_id=1, source_target_pairs={{0,32},{16,48},{32,0},{48,16},{64,96},{80,112},{96,64},{112,80},{1... | collective-permute-start | bytes 393224 | tf_op jit(solution)/shard_map/ppermute | solution.py:18
  172.4 12.9 %collective-permute-start.27 = (bf16[3,128,256]{2,1,0:T(8,128)(2,1)S(1)}, bf16[3,128,256]{2,1,0:T(8,128)(2,1)S(1)}, u32[]{:S(2)}, u32[]{:S(2)}) collective-permute-start(bf16[3,128,256]{2,1,0:T(8,128)(2,1)S(1)} %add_convert_fusion.3), channel_id=1, source_target_pairs={{0,16},{16,0},{32,48},{48,32},{64,80},{80,64},{96,112},{112,96},{1... | collective-permute-start | bytes 589832 | tf_op jit(solution)/shard_map/ppermute | solution.py:18
  174.9 20.3 %collective-permute-start.23 = (bf16[1,256,256]{2,1,0:T(8,128)(2,1)S(1)}, bf16[1,256,256]{2,1,0:T(8,128)(2,1)S(1)}, u32[]{:S(2)}, u32[]{:S(2)}) collective-permute-start(bf16[1,256,256]{2,1,0:T(8,128)(2,1)S(1)} %add_convert_fusion.5), channel_id=1, source_target_pairs={{0,2},{1,3},{2,0},{3,1},{4,6},{5,7},{6,4},{7,5},{8,10},{9,11},{10,... | collective-permute-start | bytes 393224 | tf_op jit(solution)/shard_map/ppermute | solution.py:18
  177.4 31.9 %collective-permute-start.21 = (bf16[3,256,256]{2,1,0:T(8,128)(2,1)S(1)}, bf16[3,256,256]{2,1,0:T(8,128)(2,1)S(1)}, u32[]{:S(2)}, u32[]{:S(2)}) collective-permute-start(bf16[3,256,256]{2,1,0:T(8,128)(2,1)S(1)} %get-tuple-element.34), channel_id=1, source_target_pairs={{0,32},{16,48},{32,0},{48,16},{64,96},{80,112},{96,64},{112,80},{1... | collective-permute-start | bytes 1179656 | tf_op jit(solution)/shard_map/ppermute | solution.py:18
  185.3 15.7 %collective-permute-start.30 = (bf16[3,256,256]{2,1,0:T(8,128)(2,1)S(1)}, bf16[3,256,256]{2,1,0:T(8,128)(2,1)S(1)}, u32[]{:S(2)}, u32[]{:S(2)}) collective-permute-start(bf16[3,256,256]{2,1,0:T(8,128)(2,1)S(1)} %pad_maximum_fusion.7.refs_0_), channel_id=1, source_target_pairs={{0,12},{4,0},{8,4},{12,8},{1,13},{5,1},{9,5},{13,9},{2,14},{6,2},{... | collective-permute-start | bytes 1179656 | tf_op jit(solution)/shard_map/ppermute | solution.py:18
  187.9 13.1 %collective-permute-start.29 = (bf16[3,256,256]{2,1,0:T(8,128)(2,1)S(1)}, bf16[3,256,256]{2,1,0:T(8,128)(2,1)S(1)}, u32[]{:S(2)}, u32[]{:S(2)}) collective-permute-start(bf16[3,256,256]{2,1,0:T(8,128)(2,1)S(1)} %pad_maximum_fusion.7.refs_0_), channel_id=1, source_target_pairs={{0,4},{4,8},{8,12},{12,0},{1,5},{5,9},{9,13},{13,1},{2,6},{6,10},{... | collective-permute-start | bytes 1179656 | tf_op jit(solution)/shard_map/ppermute | solution.py:18
  191.2 17.4 %collective-permute-start.28 = (bf16[3,256,256]{2,1,0:T(8,128)(2,1)S(1)}, bf16[3,256,256]{2,1,0:T(8,128)(2,1)S(1)}, u32[]{:S(2)}, u32[]{:S(2)}) collective-permute-start(bf16[3,256,256]{2,1,0:T(8,128)(2,1)S(1)} %pad_maximum_fusion.7.refs_0_), channel_id=1, source_target_pairs={{0,8},{4,12},{8,0},{12,4},{1,9},{5,13},{9,1},{13,5},{2,10},{6,14},... | collective-permute-start | bytes 1179656 | tf_op jit(solution)/shard_map/ppermute | solution.py:18
  195.3 3.4 %collective-permute-start.24 = (bf16[2,1,256,256]{3,2,1,0:T(8,128)(2,1)S(1)}, bf16[2,1,256,256]{3,2,1,0:T(8,128)(2,1)S(1)}, u32[]{:S(2)}, u32[]{:S(2)}) collective-permute-start(bf16[2,1,256,256]{3,2,1,0:T(8,128)(2,1)S(1)} %pad_maximum_fusion.9.own), channel_id=1, source_target_pairs={{0,1},{1,0},{2,3},{3,2},{4,5},{5,4},{6,7},{7,6},{8,9},{9,8},{10,11... | collective-permute-start | bytes 786440 | tf_op jit(solution)/shard_map/ppermute | solution.py:18
  210.1 8.3 %collective-permute-start.31 = (bf16[128,1024]{1,0:T(8,128)(2,1)S(1)}, bf16[128,1024]{1,0:T(8,128)(2,1)S(1)}, u32[]{:S(2)}, u32[]{:S(2)}) collective-permute-start(bf16[128,1024]{1,0:T(8,128)(2,1)S(1)} %get-tuple-element.40), channel_id=1, source_target_pairs={{0,64},{16,80},{32,96},{48,112},{64,0},{80,16},{96,32},{112,48},{1... | collective-permute-start | bytes 786440 | tf_op jit(solution)/shard_map/ppermute | solution.py:18
  (4 other events, 28.4 us)
